TPU v7x, 32 devices: a whole 2x2x4 slice. The times are simulated.
32 devices in a mesh: row: 8 (over z, x), col: 4 (over y, core).
Axes of the slice: x: 2, y: 2, z: 4, core: 2. Of those that a mesh axis runs over, the one named last changes fastest.
Arguments:
- links: bfloat16 [2048, 2048], P('row', 'col'), may hold values from 0 to 3, as said below
- tiles: int32 [16, 16], P('row', 'col'), may hold values from 0 to 1
- local_links: bfloat16 [2048, 64], P(('col', 'row')), may hold values from 0 to 2, as said below
- host_ids: int32 [2048], replicated, may hold values from 0 to 127, as said below
- dangling: int32 [2048], replicated, may hold values 0 or 1
- teleport: float32 [2048, 128], P(('col', 'row')), may hold values from 0.1 to 10
Outputs:
- ranks: float32 [2048, 128], P(('row', 'col'))
Inputs may be any that keep to these rules, and one draw needn't show every extreme that they name: `links`: small whole link counts. `local_links`: small whole link counts. `host_ids`: the pages of piece q form exactly 4 hosts, numbered q * 4 onwards in page order; each host is a run of consecutive pages.
All inputs are finite; a program needn't handle non-finite values.
Results may differ from a plain program's by a relative error of at most 0.0045.
Values may be sent and summed in bfloat16 or wider, within the bound.
No kernel may reach another device: no remote copies, remote signals or barrier semaphores. Data moves between devices by JAX's collectives and lax.ppermute only.
A program may use at most 64 MiB of HBM per device.

v0:
```python
import jax
import jax.numpy as jnp
from jax import lax
from jax.sharding import PartitionSpec as P

HOSTS_PIECE = 4
LOCAL_ITERS = 2
HOST_ITERS = 3


damping = 0.85
highest = lax.Precision.HIGHEST


def local_ranks(local_links, hosts, dangling, teleport, first_host):
    member = (
        (hosts - first_host[:, None])[:, :, None]
        == jnp.arange(HOSTS_PIECE, dtype=jnp.int32)[None, None, :]
    ).astype(jnp.float32)
    same = (hosts[:, :, None] == hosts[:, None, :]).astype(jnp.float32)
    follow = (1 - dangling).astype(jnp.float32)
    inside = local_links.astype(jnp.float32) * same * follow[:, None, :]
    inward = jnp.sum(inside, axis=1)
    live = inward > 0
    inverse = jnp.where(live, 1.0 / jnp.where(live, inward, 1.0), 0.0)
    sizes = jnp.sum(member, axis=1)
    page_size = jnp.einsum("npg,ng->np", member, sizes, precision=highest)
    host_tele = jnp.einsum("npg,npk->ngk", member, teleport, precision=highest)
    page_tele = jnp.einsum("npg,ngk->npk", member, host_tele, precision=highest)
    restart = page_size[:, :, None] * teleport / page_tele
    ranks = jnp.ones(teleport.shape, jnp.float32)
    for step in range(LOCAL_ITERS):
        flow = jnp.einsum("npq,nqk->npk", inside, ranks * inverse[:, :, None], precision=highest)
        lost = jnp.einsum(
            "npg,npk->ngk", member, jnp.where(live[:, :, None], 0.0, ranks), precision=highest
        )
        spread = jnp.einsum("npg,ngk->npk", member, lost, precision=highest) / page_size[:, :, None]
        ranks = damping * (flow + spread) + (1 - damping) * restart
    return (ranks, member, inside, inward)


def share_ranks(values):
    return lax.all_gather(values, "row", axis=0, tiled=True)


def host_member(hosts, first):
    return (
        (hosts - first[:, None])[:, :, None]
        == jnp.arange(HOSTS_PIECE, dtype=jnp.int32)[None, None, :]
    ).astype(jnp.float32)


def on_device(links, tiles, local_links, host_ids, dangling, teleport):
    row_count = lax.axis_size("row")
    column_count = lax.axis_size("col")
    row = lax.axis_index("row")
    column = lax.axis_index("col")
    piece = local_links.shape[0]
    height, width = links.shape
    tile = height // tiles.shape[0]
    pages = piece * row_count * column_count
    hosts_all = HOSTS_PIECE * row_count * column_count
    column_hosts = HOSTS_PIECE * row_count
    row_hosts = HOSTS_PIECE * column_count
    owner = column * row_count + row
    row_start = row * height
    column_start = column * width
    host_rows = lax.dynamic_slice_in_dim(host_ids, row_start, height, 0)
    host_columns = lax.dynamic_slice_in_dim(host_ids, column_start, width, 0)
    host_own = lax.dynamic_slice_in_dim(host_ids, owner * piece, piece, 0)
    ignored_columns = lax.dynamic_slice_in_dim(dangling, column_start, width, 0)
    ignored_own = lax.dynamic_slice_in_dim(dangling, owner * piece, piece, 0)
    stored = jnp.broadcast_to(
        (tiles > 0)[:, None, :, None], (tiles.shape[0], tile, tiles.shape[1], tile)
    ).reshape(height, width)
    valid = stored & (host_rows[:, None] != host_columns[None, :]) & (ignored_columns == 0)[None, :]
    between = jnp.where(valid, links, jnp.zeros((), jnp.bfloat16))
    outward = lax.psum(jnp.sum(between, axis=0, dtype=jnp.float32), "row")
    ranks, member, inside, inward = local_ranks(
        local_links[None],
        host_own[None],
        ignored_own[None],
        teleport[None],
        (owner * HOSTS_PIECE)[None],
    )
    ranks = ranks[0]
    member = member[0]
    inside = inside[0]
    inward = inward[0]
    degree = inward + lax.dynamic_slice_in_dim(outward, row * piece, piece, 0)
    has_out = degree > 0
    inverse_degree = jnp.where(has_out, 1.0 / jnp.where(has_out, degree, 1.0), 0.0)
    scaled = (ranks * inverse_degree[:, None]).astype(jnp.bfloat16)
    column_first = (column * row_count + jnp.arange(row_count, dtype=jnp.int32)) * HOSTS_PIECE
    column_member = host_member(host_columns.reshape(row_count, piece), column_first)
    early = lax.all_gather(scaled, "row", axis=0, tiled=True)
    means = jnp.mean(early.astype(jnp.float32), axis=1).astype(jnp.bfloat16)
    spread_weight = (
        column_member * means.astype(jnp.float32).reshape(row_count, piece)[:, :, None]
    ).astype(jnp.bfloat16)
    to_hosts = jnp.einsum(
        "iqj,qjh->iqh",
        between.reshape(height, row_count, piece),
        spread_weight,
        preferred_element_type=jnp.float32,
    )
    to_hosts = to_hosts.reshape(column_count, piece, column_hosts)
    row_first = (row * column_count + jnp.arange(column_count, dtype=jnp.int32)) * HOSTS_PIECE
    row_member = host_member(host_rows.reshape(column_count, piece), row_first)
    weights = jnp.einsum("pig,pih->pgh", row_member, to_hosts, precision=highest).reshape(
        row_hosts, column_hosts
    )
    out_weight = lax.psum(jnp.sum(weights, axis=0), "row")
    linked = out_weight > 0
    norm = jnp.where(linked[None, :], weights / jnp.where(linked, out_weight, 1.0)[None, :], 0.0)
    loose = jnp.where(linked, 0.0, 1.0)
    host_rank = jnp.ones((hosts_all,), jnp.float32)
    for step in range(HOST_ITERS):
        column_rank = lax.dynamic_slice_in_dim(host_rank, column * column_hosts, column_hosts, 0)
        partial_rank = (
            jnp.dot(norm, column_rank, precision=highest) + jnp.sum(loose * column_rank) / hosts_all
        )
        fresh = damping * lax.psum(partial_rank, "col") + (1 - damping)
        host_rank = share_ranks(fresh)
    page_weight = jnp.dot(
        member,
        lax.dynamic_slice_in_dim(host_rank, owner * HOSTS_PIECE, HOSTS_PIECE, 0),
        precision=highest,
    )
    start_rank = ranks * page_weight[:, None]
    sources = (scaled.astype(jnp.float32) * page_weight[:, None]).astype(jnp.bfloat16)
    lost_mass = jnp.sum(jnp.where(has_out[:, None], 0.0, start_rank), axis=0)
    mass, tele_total = lax.psum((lost_mass, jnp.sum(teleport, axis=0)), ("row", "col"))
    own = damping * jnp.dot(inside, sources.astype(jnp.float32), precision=highest)
    own = (own + (1 - damping) * pages * teleport / tele_total).astype(jnp.bfloat16)
    own_columns = lax.all_gather(own, "row", axis=0, tiled=True)
    column_rank = lax.dynamic_slice_in_dim(
        host_rank, column * column_hosts, column_hosts, 0
    ).reshape(row_count, HOSTS_PIECE)
    column_weight = jnp.einsum("pjh,ph->pj", column_member, column_rank, precision=highest).reshape(
        width
    )
    source_columns = (early.astype(jnp.float32) * column_weight[:, None]).astype(jnp.bfloat16)
    offset = row_start - column_start
    diagonal = (offset >= 0) & (offset < width)
    base = jnp.clip(offset, 0, width - height)
    flowing = damping * jnp.dot(between, source_columns, preferred_element_type=jnp.float32)
    mine = lax.dynamic_slice_in_dim(own_columns, base, lax.axis_size("col") * piece, 0).astype(
        jnp.float32
    )
    flows = lax.psum_scatter(
        flowing + jnp.where(diagonal, mine, 0.0), "col", scatter_dimension=0, tiled=True
    )
    return flows + damping * mass / pages


def solution(mesh):
    return jax.shard_map(
        on_device,
        mesh=mesh,
        in_specs=(
            P("row", "col"),
            P("row", "col"),
            P(("col", "row"), None),
            P(),
            P(),
            P(("col", "row"), None),
        ),
        out_specs=P(("row", "col"), None),
        check_vma=False,
    )
```

profile of v0, /device:TPU:0, one launch (start us, length us, event | category | flops | bytes accessed | tf_op | source)
XLA Modules:
  0.0 263.6 jit_solution(2284809991217232889)
XLA Ops:
  6.5 0.8 dynamic_slice.34
  7.3 0.8 dynamic_slice.35
  8.1 0.8 dynamic-slice_compare_fusion
  8.8 0.1 broadcast_in_dim.59
  9.0 1.2 convert_reduce_fusion
  10.2 23.1 %psum.49 = f32[512]{0:T(512)S(1)} all-reduce(f32[512]{0:T(512)S(1)} %get-tuple-element.7), channel_id=1, replica_groups=mesh['row'=8,'col'=4] {'row'}, use_global_device_ids=true, to_apply=%region_3.4 | all-reduce | flops 512 | bytes 4096 | tf_op jit(solution)/shard_map/psum | solution.py:78
  33.3 0.8 broadcast_subtract_fusion.2
  34.1 0.1 fusion.27
  34.2 0.1 divide_select_fusion.1
  34.3 0.1 broadcast_compare_fusion.2
  34.4 0.1 reshape.341
  34.4 0.1 reshape.342
  34.5 0.2 fusion.26
  34.8 0.1 convert_reduce_fusion.2
  34.9 0.3 fusion.25
  35.1 0.2 convolution_bitcast_fusion.5
  35.3 0.6 copy-done
  35.9 0.2 fusion.24
  36.2 0.2 fusion.5
  36.4 0.2 fusion.8
  36.6 0.2 fusion.22
  36.9 0.3 fusion.20
  37.1 0.2 multiply_convert_fusion.1
  37.4 30.5 %all_gather.15 = bf16[512,128]{1,0:T(8,128)(2,1)S(1)} all-gather(bf16[64,128]{1,0:T(8,128)(2,1)S(1)} %get-tuple-element.18), channel_id=1, replica_groups=mesh['row'=8,'col'=4] {'row'}, dimensions={0}, use_global_device_ids=true | all-gather | bytes 147456 | tf_op jit(solution)/shard_map/all_gather | solution.py:96
  67.9 0.1 convert_reduce_fusion.1
  68.0 0.1 reshape.347
  68.1 0.1 copy.14
  68.2 0.1 broadcast_subtract_fusion
  68.3 0.1 convolution_bitcast_fusion
  68.5 0.1 reshape.344
  68.6 0.1 broadcast_subtract_fusion.1
  68.6 0.2 fusion.78
  68.8 17.1 %psum.50 = f32[32]{0:T(128)S(1)} all-reduce(f32[32]{0:T(128)S(1)} %get-tuple-element.20), channel_id=1, replica_groups=mesh['row'=8,'col'=4] {'row'}, use_global_device_ids=true, to_apply=%region_6.7 | all-reduce | flops 32 | bytes 256 | tf_op jit(solution)/shard_map/psum | solution.py:113
  86.0 0.6 broadcast_select_fusion.1
  87.2 0.1 fusion.12
  87.4 5.6 %psum.51 = f32[16]{0:T(128)S(1)} all-reduce(f32[16]{0:T(128)S(1)} %fusion.12), channel_id=1, replica_groups=mesh['row'=8,'col'=4] {'col'}, use_global_device_ids=true, to_apply=%region_8.9 | all-reduce | flops 16 | bytes 128 | tf_op jit(solution)/shard_map/psum | solution.py:123
  93.0 0.7 copy-done.3
  93.7 0.6 dynamic-slice
  94.9 0.1 add_dynamic-update-slice_fusion.2
  95.0 19.1 %all-reduce = f32[128]{0:T(128)S(1)} all-reduce(f32[128]{0:T(128)S(1)} %add_dynamic-update-slice_fusion.2), channel_id=1, replica_groups=mesh['row'=8,'col'=4] {'row'}, use_global_device_ids=true, to_apply=%add | all-reduce | flops 128 | bytes 1024
  114.1 0.8 multiply_reduce_fusion.1
  115.6 0.2 fusion.11
  115.8 5.6 %psum.52 = f32[16]{0:T(128)S(1)} all-reduce(f32[16]{0:T(128)S(1)} %fusion.11), channel_id=1, replica_groups=mesh['row'=8,'col'=4] {'col'}, use_global_device_ids=true, to_apply=%region_10.11 | all-reduce | flops 16 | bytes 128 | tf_op jit(solution)/shard_map/psum | solution.py:123
  121.4 0.1 add_dynamic-update-slice_fusion.1
  121.5 17.1 %all-reduce.1 = f32[128]{0:T(128)S(1)} all-reduce(f32[128]{0:T(128)S(1)} %add_dynamic-update-slice_fusion.1), channel_id=1, replica_groups=mesh['row'=8,'col'=4] {'row'}, use_global_device_ids=true, to_apply=%add.1 | all-reduce | flops 128 | bytes 1024
  138.6 0.8 multiply_reduce_fusion
  140.1 0.2 fusion.10
  140.3 5.6 %psum.53 = f32[16]{0:T(128)S(1)} all-reduce(f32[16]{0:T(128)S(1)} %fusion.10), channel_id=1, replica_groups=mesh['row'=8,'col'=4] {'col'}, use_global_device_ids=true, to_apply=%region_12.13 | all-reduce | flops 16 | bytes 128 | tf_op jit(solution)/shard_map/psum | solution.py:123
  145.9 0.1 add_dynamic-update-slice_fusion
  146.0 19.1 %all-reduce.2 = f32[128]{0:T(128)S(1)} all-reduce(f32[128]{0:T(128)S(1)} %add_dynamic-update-slice_fusion), channel_id=1, replica_groups=mesh['row'=8,'col'=4] {'row'}, use_global_device_ids=true, to_apply=%add.2 | all-reduce | flops 128 | bytes 1024
  165.2 0.1 dynamic_slice.42
  165.2 0.2 convolution_bitcast_fusion.1
  165.4 0.1 reduce_sum.98
  165.5 0.1 select_reduce_fusion
  165.6 36.9 %all-reduce.3 = (f32[128]{0:T(128)S(1)}, f32[128]{0:T(128)S(1)}) all-reduce(f32[128]{0:T(128)S(1)} %reduce_sum.98, f32[128]{0:T(128)S(1)} %select_reduce_fusion), channel_id=1, replica_groups=mesh['row'=8,'col'=4] {'row','col'}, use_global_device_ids=true, to_apply=%region_14.15 | all-reduce | flops 256 | bytes 2048 | tf_op jit(solution)/shard_map/psum | solution.py:133
  202.4 0.2 fusion.9
  202.7 30.5 %all_gather.19 = bf16[512,128]{1,0:T(8,128)(2,1)S(1)} all-gather(bf16[64,128]{1,0:T(8,128)(2,1)S(1)} %fusion.9), channel_id=1, replica_groups=mesh['row'=8,'col'=4] {'row'}, dimensions={0}, use_global_device_ids=true | all-gather | bytes 147456 | tf_op jit(solution)/shard_map/all_gather | solution.py:136
  233.2 0.1 reshape.371
  233.3 0.2 fusion.32
  233.4 0.1 mul.192
  233.5 1.0 fusion
  234.5 0.0 reduce-scatter.2.cloned.1.call-update
  234.5 20.9 %reduce-scatter.2.cloned.1.call-done = f32[64,128]{1,0:T(8,128)} async-done(((f32[256,128]{1,0:T(8,128)}), f32[64,128]{1,0:T(8,128)}) %reduce-scatter.2.cloned.1.call-update) | async-done | bytes 32784 | tf_op jit(solution)/shard_map/reduce_scatter | solution.py:151
  255.4 1.4 broadcast_add_fusion
  (16 shorter events, 0.1 us)
Async XLA Ops:
  6.5 248.9 %reduce-scatter.2.cloned.1.call-start = ((), (), s32[]{:S(2)}) async-start(), calls=%async_computation.1 | async-start | bytes 163840 | tf_op jit(solution)/shard_map/reduce_scatter | solution.py:151
  8.1 0.8 copy-start.2
  10.2 23.9 %copy-start.1 = (bf16[64,64]{1,0:T(8,128)(2,1)S(1)}, bf16[64,64]{1,0:T(8,128)(2,1)}, u32[]{:S(2)}) copy-start(bf16[64,64]{1,0:T(8,128)(2,1)} %param.8) | copy-start | bytes 24580
  35.1 0.8 copy-start
  93.0 0.7 copy-start.3
Sparse Core Ops, SparseCore 0:
  234.6 20.7 reduce-scatter.1
where the time goes:
time: 264 us
  blocking collectives  210 us (80%)
  waiting for transfers between devices  20.9 us (8%)
  between operations  16.2 us (6%)
  other arithmetic  7.34 us (3%)
  matrix products  4.49 us (2%)
  local copies, waits for them, and re-layouts  4.19 us (2%)
    unnamed x3, blocking collectives  55.4 us
    psum x1, blocking collectives, on_device(): lax.psum((lost_mass, jnp.sum(teleport, axis=0)), ('row', 'col'))  36.9 us
    all_gather x1, blocking collectives, on_device(): early = lax.all_gather(scaled, 'row', axis=0, tiled=True)  30.5 us
    all_gather x1, blocking collectives, on_device(): own_columns = lax.all_gather(own, 'row', axis=0, tiled=True)  30.5 us
    psum x1, blocking collectives, on_device(): outward = lax.psum(jnp.sum(between, axis=0, dtype=jnp.float32), 'row')  23.1 us
    reduce_scatter x1, waiting for transfers between devices, on_device(): lax.psum_scatter(flowing + jnp.where(diagonal, mine, 0.0), 'col', scatter...  20.9 us
    psum x1, blocking collectives, on_device(): out_weight = lax.psum(jnp.sum(weights, axis=0), 'row')  17.1 us
    psum x3, blocking collectives, on_device(): fresh = damping * lax.psum(partial_rank, 'col') + (1 - damping)  16.9 us
  transfers between devices with their start and end apart: 1, of which 1 were waited for; matrix products, arithmetic and copies ran while one was open for 0% of the time, Pallas kernels for 0%

commit v1 on v0

v1 whole, which is shorter than its diff:
```python
import functools

import jax
import jax.numpy as jnp
from jax import lax
from jax.experimental import pallas as pl
from jax.experimental.pallas import tpu as pltpu
from jax.sharding import PartitionSpec as P

HOSTS_PIECE = 4
LOCAL_ITERS = 2
HOST_ITERS = 3
LANES = 128

damping = 0.85
f32 = jnp.float32
bf16 = jnp.bfloat16

VMEM = pl.BlockSpec(memory_space=pltpu.VMEM)
SMEM = pl.BlockSpec(memory_space=pltpu.SMEM)


def iota(shape, axis):
    return lax.broadcasted_iota(jnp.int32, shape, axis)


def mm(a, b):
    return jnp.dot(a, b, preferred_element_type=f32)


def mm_nt(a, b):
    return lax.dot_general(a, b, (((1,), (1,)), ((), ())), preferred_element_type=f32)


def mm_tn(a, b):
    return lax.dot_general(a, b, (((0,), (0,)), ((), ())), preferred_element_type=f32)


def split(x):
    high = x.astype(bf16)
    return high, (x - high.astype(f32)).astype(bf16)


def members(hosts_row, first, count):
    return hosts_row == first + iota((count, hosts_row.shape[1]), 0)


class Sizes:
    def __init__(self, rows, cols, links, tiles, local_links, teleport, pages):
        self.rows, self.cols, self.pages = rows, cols, pages
        self.height, self.width = links
        self.piece = local_links[0]
        self.topics = teleport[1]
        self.tile = self.height // tiles[0]
        self.tile_rows, self.units = tiles
        self.pair = self.tile // self.piece
        self.unit_hosts = self.pair * HOSTS_PIECE
        self.hosts = HOSTS_PIECE * rows * cols
        self.column_hosts = HOSTS_PIECE * rows
        self.row_hosts = HOSTS_PIECE * cols
        self.packed = self.piece * self.piece // LANES
        self.at_links = self.piece
        self.at_counts = self.at_links + self.packed
        self.payload = self.at_counts + self.units * self.row_hosts


def gather_kernel(s, tiles_ref, links_ref, hosts_ref, dangling_ref, local_ref, teleport_ref, out_ref):
    row, column = lax.axis_index("row"), lax.axis_index("col")
    counts = [[] for _ in range(s.units)]
    for a in range(s.tile_rows):
        tile_row = row * s.tile_rows + a
        first = tile_row * s.unit_hosts
        member = members(hosts_ref[pl.ds(tile_row, 1), :], first, s.unit_hosts)
        sums = mm(member.astype(bf16), links_ref[a * s.tile : (a + 1) * s.tile, :])
        for b in range(s.units):
            unit = column * s.units + b
            target = hosts_ref[pl.ds(unit, 1), :]
            valid = ~members(target, first, s.unit_hosts) & (dangling_ref[pl.ds(unit, 1), :] == 0)
            stored = (tiles_ref[a, b] > 0).astype(f32)
            part = sums[:, b * s.tile : (b + 1) * s.tile]
            counts[b].append(jnp.where(valid, part, 0.0) * stored)
    local = local_ref[...].astype(f32)
    half = s.piece // 2
    packed = jnp.concatenate([local[:half], local[half:]], axis=1).astype(bf16)
    values = jnp.concatenate(
        [teleport_ref[...].astype(bf16), packed]
        + [jnp.concatenate(c, axis=0).astype(bf16) for c in counts],
        axis=0,
    )
    for n in range(s.rows):
        out_ref[n] = values


def unpack_links(s, buffer_ref, first):
    parts = []
    low = iota((s.packed, LANES), 1) < s.piece
    for q in range(s.pair):
        packed = buffer_ref[first + q, s.at_links : s.at_counts, :].astype(f32)
        rolled = pltpu.roll(packed, s.piece, 1)
        parts += [jnp.where(low, packed, rolled), jnp.where(low, rolled, packed)]
    return jnp.concatenate(parts, axis=0)


def unpack_teleport(s, buffer_ref, first):
    return jnp.concatenate([buffer_ref[first + q, : s.piece, :] for q in range(s.pair)], axis=0)


def rank_kernel(s, buffer_ref, hosts_ref, dangling_ref, norm_ref, local_ref, aux_ref):
    column = lax.axis_index("col")
    ones = jnp.ones((s.tile, LANES), bf16)
    total = jnp.zeros((8, s.topics), f32)
    inverses, deads = [], []
    for m in range(s.units):
        unit = column * s.units + m
        hosts = hosts_ref[pl.ds(unit, 1), :]
        keep = (dangling_ref[pl.ds(unit, 1), :] == 0).astype(f32)
        member = members(hosts, unit * s.unit_hosts, s.unit_hosts).astype(f32)
        memberb = member.astype(bf16)
        same = mm_tn(memberb, memberb)
        sameb = same.astype(bf16)
        inside = unpack_links(s, buffer_ref, s.pair * m) * same * keep
        inward = jnp.sum(inside, axis=0, keepdims=True)
        size = jnp.sum(same, axis=0, keepdims=True)
        live = inward > 0
        step = inside * jnp.where(live, 1.0 / jnp.where(live, inward, 1.0), 0.0)
        step = step + same * jnp.where(live, 0.0, 1.0 / size)
        high, low = split(step)
        teleport = unpack_teleport(s, buffer_ref, s.pair * m)
        total = total + mm(ones[:8], teleport)
        restart = mm(sameb, ones) * teleport.astype(f32) / mm(sameb, teleport)
        ranks = damping * (mm(high, ones) + mm(low, ones)) + (1 - damping) * restart
        for _ in range(LOCAL_ITERS - 1):
            ranks_high, ranks_low = split(ranks)
            flow = mm(high, ranks_high) + mm(high, ranks_low) + mm(low, ranks_high)
            ranks = damping * flow + (1 - damping) * restart
        ranks_high, ranks_low = split(ranks)
        local_ref[m * s.tile : (m + 1) * s.tile, :] = ranks_high
        start = s.at_counts + m * s.row_hosts
        counts = jnp.concatenate(
            [buffer_ref[n, start : start + s.row_hosts, :] for n in range(s.rows)], axis=0
        )
        outward = mm(jnp.ones((8, s.hosts), bf16), counts)[:1]
        degree = inward + outward
        has_out = degree > 0
        inverse = jnp.where(has_out, 1.0 / jnp.where(has_out, degree, 1.0), 0.0)
        sums = mm_nt(ones[:8, : s.topics], ranks_high) + mm_nt(ones[:8, : s.topics], ranks_low)
        means = sums[:1] * (1.0 / s.topics) * inverse
        weights = mm_nt((member * means).astype(bf16), counts)
        out = jnp.sum(weights, axis=1, keepdims=True)
        linked = out > 0
        norm = jnp.where(linked, weights / jnp.where(linked, out, 1.0), 1.0 / s.hosts)
        norm_ref[m * s.unit_hosts : (m + 1) * s.unit_hosts, :] = norm
        inverses.append(inverse)
        deads.append(jnp.where(has_out, 0.0, 1.0 / s.pages))
    norm_ref[s.column_hosts :, : s.topics] = total
    aux_ref[...] = jnp.concatenate(inverses + deads, axis=0)


def edges_kernel(s, tiles_ref, links_ref, buffer_ref, hosts_ref, aux_ref, out_ref):
    row, column = lax.axis_index("row"), lax.axis_index("col")
    first = row * s.tile_rows - column * s.units
    for a in range(s.tile_rows):
        rows = slice(a * s.tile, (a + 1) * s.tile)
        for b in range(s.units):
            lanes = slice(b * s.tile, (b + 1) * s.tile)
            inverse = aux_ref[b : b + 1, :]
            dead = aux_ref[s.units + b : s.units + b + 1, :]
            scale = inverse * (tiles_ref[a, b] > 0).astype(f32)
            out_ref[rows, lanes] = links_ref[rows, lanes].astype(f32) * scale + dead

            @pl.when(first + a == b)
            def _():
                unit = column * s.units + b
                memberb = members(hosts_ref[pl.ds(unit, 1), :], unit * s.unit_hosts, s.unit_hosts)
                memberb = memberb.astype(bf16)
                same = mm_tn(memberb, memberb) > 0
                inside = unpack_links(s, buffer_ref, s.pair * b) * inverse
                across = links_ref[rows, lanes].astype(f32) * scale
                out_ref[rows, lanes] = jnp.where(same, inside, across) + dead


def flow_kernel(s, *refs):
    norms, (edges_ref, local_ref, buffer_ref, hosts_ref, out_ref, full_ref) = refs[: s.cols], refs[s.cols :]
    row, column = lax.axis_index("row"), lax.axis_index("col")
    total = jnp.zeros((8, s.topics), f32)
    for k in range(s.cols):
        at = pl.multiple_of((column ^ k) * s.column_hosts, s.column_hosts)
        full_ref[pl.ds(at, s.column_hosts), :] = norms[k][: s.column_hosts, :]
        total = total + norms[k][s.column_hosts :, : s.topics]
    norm = full_ref[...]
    norm_high, norm_low = split(norm)

    def three(x):
        high = x.astype(bf16).astype(f32)
        rest = x - high
        middle = rest.astype(bf16).astype(f32)
        where = iota((8, x.shape[1]), 0)
        parts = jnp.where(where == 0, high, jnp.where(where == 1, middle, rest - middle))
        return jnp.where(where < 3, parts, 0.0).astype(bf16)

    rank = damping * jnp.sum(norm, axis=0, keepdims=True) + (1 - damping)
    for _ in range(HOST_ITERS - 1):
        parts = three(rank)
        fresh = mm(parts, norm_high) + mm(parts, norm_low)
        rank = damping * jnp.sum(fresh, axis=0, keepdims=True) + (1 - damping)
    parts = three(rank)
    scales = []
    for b in range(s.units):
        hosts = hosts_ref[pl.ds(column * s.units + b, 1), :]
        chosen = mm(parts, members(hosts, 0, s.hosts).astype(bf16))
        scales.append(jnp.sum(chosen, axis=0, keepdims=True))
    scale = jnp.concatenate(scales, axis=1)
    tele_scale = (1 - damping) * s.pages / total[:1]
    first = row * s.cols - column * s.rows
    diagonal = (first >= 0) & (first < s.rows)
    for place, k in enumerate(exchange_order(s.cols)):
        chunk = column ^ k
        at = pl.multiple_of(chunk * s.piece, s.piece)
        weighted = (edges_ref[pl.ds(at, s.piece), :] * scale).astype(bf16)
        flow = damping * mm(weighted, local_ref[...])
        out_ref[place * s.piece : (place + 1) * s.piece, :] = flow

        @pl.when(diagonal)
        def _():
            own = buffer_ref[first + chunk, : s.piece, :].astype(f32) * tele_scale
            out_ref[place * s.piece : (place + 1) * s.piece, :] = flow + own


def exchange_order(count):
    bits = count.bit_length() - 1
    return [int(format(i, f"0{bits}b")[::-1], 2) if bits else 0 for i in range(count)]


def swap(x, count, bit):
    return lax.ppermute(x, "col", [(i, i ^ bit) for i in range(count)])


def on_device(links, tiles, local_links, host_ids, dangling, teleport):
    rows, cols = lax.axis_size("row"), lax.axis_size("col")
    pages = host_ids.shape[0]
    s = Sizes(rows, cols, links.shape, tiles.shape, local_links.shape, teleport.shape, pages)
    hosts = host_ids.reshape(pages // LANES, LANES)
    ignored = dangling.reshape(pages // LANES, LANES)
    sent = pl.pallas_call(
        functools.partial(gather_kernel, s),
        out_shape=jax.ShapeDtypeStruct((rows, s.payload, LANES), bf16),
        in_specs=[SMEM] + [VMEM] * 5,
        out_specs=VMEM,
    )(tiles, links, hosts, ignored, local_links, teleport)
    held = lax.all_to_all(sent, "row", 0, 0, tiled=True)
    norm, local, aux = pl.pallas_call(
        functools.partial(rank_kernel, s),
        out_shape=(
            jax.ShapeDtypeStruct((s.column_hosts + 8, s.hosts), f32),
            jax.ShapeDtypeStruct((s.width, s.topics), bf16),
            jax.ShapeDtypeStruct((2 * s.units, LANES), f32),
        ),
        in_specs=[VMEM] * 3,
        out_specs=(VMEM,) * 3,
    )(held, hosts, ignored)
    norms = {0: norm}
    bit = cols // 2
    while bit:
        norms.update({k ^ bit: swap(v, cols, bit) for k, v in norms.items()})
        bit //= 2
    edges = pl.pallas_call(
        functools.partial(edges_kernel, s),
        out_shape=jax.ShapeDtypeStruct((s.height, s.width), f32),
        in_specs=[SMEM] + [VMEM] * 4,
        out_specs=VMEM,
        cost_estimate=pl.CostEstimate(flops=10**6, bytes_accessed=10**6, transcendentals=0),
    )(tiles, links, held, hosts, aux)
    flows = pl.pallas_call(
        functools.partial(flow_kernel, s),
        out_shape=jax.ShapeDtypeStruct((s.height, s.topics), f32),
        in_specs=[VMEM] * (cols + 4),
        out_specs=VMEM,
        scratch_shapes=[pltpu.VMEM((s.hosts, s.hosts), f32)],
    )(*(norms[k] for k in range(cols)), edges, local, held, hosts)
    bit = 1
    while bit < cols:
        half = flows.shape[0] // 2
        flows = flows[:half] + swap(flows[half:], cols, bit)
        bit *= 2
    return flows


def solution(mesh):
    return jax.shard_map(
        on_device,
        mesh=mesh,
        in_specs=(
            P("row", "col"),
            P("row", "col"),
            P(("col", "row"), None),
            P(),
            P(),
            P(("col", "row"), None),
        ),
        out_specs=P(("row", "col"), None),
        check_vma=False,
    )
```

time: 264 us -> 41.8 us (0.16)
  blocking collectives: 210 us -> 18.3 us
  between operations: 16.2 us -> 0.04 us
  waiting for transfers between devices: 20.9 us -> 6.2 us
  Pallas kernels: 0 us -> 11.8 us
  other arithmetic: 7.34 us -> 0.63 us
  matrix products: 4.49 us -> 0 us
  starting transfers between devices: 0.01 us -> 3.03 us
  local copies, waits for them, and re-layouts: 4.19 us -> 1.52 us
    psum x6 -> x0, blocking collectives: 94 us -> none  [the longest x1 36.9 us: on_device(): lax.psum((lost_mass, jnp.sum(teleport, axis=0)), ('row', 'col'))]
    all_gather x2 -> x0, blocking collectives: 61 us -> none  [the longest x1 30.5 us: on_device(): early = lax.all_gather(scaled, 'row', axis=0, tiled=True)]
    unnamed x3 -> x0, blocking collectives: 55.4 us -> none
    reduce_scatter x1 -> x0, waiting for transfers between devices: 20.9 us -> none  [on_device(): lax.psum_scatter(flowing + jnp.where(diagonal, mine, 0.0), 'col', scatter...]
    all_to_all x0 -> x1, blocking collectives: none -> 18.3 us  [on_device(): held = lax.all_to_all(sent, 'row', 0, 0, tiled=True)]
    pallas_call x0 -> x4, Pallas kernels: none -> 11.8 us  [the longest x1 4.52 us: on_device(): pl.pallas_call(functools.partial(rank_kernel, s), out_shape=(jax.ShapeDty...]
    ppermute x0 -> x5, waiting for transfers between devices: none -> 6.2 us  [swap(): return lax.ppermute(x, 'col', [(i, i ^ bit) for i in range(count)])]
    dot_general x18 -> x0, matrix products: 4.49 us -> none  [the longest x1 0.97 us: on_device(): jnp.dot(between, source_columns, preferred_element_type=jnp.float32)]
  transfers between devices with their start and end apart: 1 -> 5, of which waited for: 1 -> 3; matrix products, arithmetic and copies ran while one was open for 0% -> 0% of each run, Pallas kernels for 0% -> 6%
where the time goes in v1:
time: 41.8 us; the launch traced here: 41.5 us
  blocking collectives  18.3 us (44%)
  Pallas kernels  11.8 us (28%)
  waiting for transfers between devices  6.2 us (15%)
  starting transfers between devices  3.03 us (7%)
  local copies, waits for them, and re-layouts  1.52 us (4%)
  other arithmetic  0.63 us (2%)
    all_to_all x1, blocking collectives, on_device(): held = lax.all_to_all(sent, 'row', 0, 0, tiled=True)  18.3 us
    ppermute x5, waiting for transfers between devices, swap(): return lax.ppermute(x, 'col', [(i, i ^ bit) for i in range(count)])  6.2 us
    pallas_call x1, Pallas kernels, on_device(): pl.pallas_call(functools.partial(rank_kernel, s), out_shape=(jax.ShapeDty...  4.52 us
    ppermute x5, starting transfers between devices, swap(): return lax.ppermute(x, 'col', [(i, i ^ bit) for i in range(count)])  3.03 us
    pallas_call x1, Pallas kernels, on_device(): pl.pallas_call(functools.partial(flow_kernel, s), out_shape=jax.ShapeDtyp...  3.01 us
    pallas_call x1, Pallas kernels, on_device(): pl.pallas_call(functools.partial(edges_kernel, s), out_shape=jax.ShapeDty...  2.37 us
    pallas_call x1, Pallas kernels, on_device(): pl.pallas_call(functools.partial(gather_kernel, s), out_shape=jax.ShapeDt...  1.87 us
    slice x2, local copies, waits for them, and re-layouts, on_device(): flows = flows[:half] + swap(flows[half:], cols, bit)  0.92 us
  transfers between devices with their start and end apart: 5, of which 3 were waited for; matrix products, arithmetic and copies ran while one was open for 0% of the time, Pallas kernels for 6%

profile of v1, /device:TPU:0, one launch (start us, length us, event | category | flops | bytes accessed | tf_op | source)
XLA Modules:
  0.0 41.5 jit_solution(6672566514695402298)
XLA Ops:
  0.0 1.9 %shard_map.64 = bf16[8,160,128]{2,1,0:T(8,128)(2,1)} custom-call(s32[2,4]{1,0:T(2,128)} %tiles_ref.3, bf16[256,512]{1,0:T(8,128)(2,1)} %links_ref.3, s32[16,128]{1,0:T(8,128)} %bitcast.2, s32[16,128]{1,0:T(8,128)} %bitcast.6, bf16[64,64]{1,0:T(8,128)(2,1)} %local_ref.1, f32[64,128]{1,0:T(8,128)} %teleport_ref.1), custom_call_target="tpu_custom_call" | custom-call | tf_op jit(solution)/shard_map/pallas_call | solution.py:244
  1.9 18.3 %all_to_all.5.buffer_ref.refs_6_ = bf16[8,160,128]{2,1,0:T(8,128)(2,1)} all-to-all(bf16[8,160,128]{2,1,0:T(8,128)(2,1)} %shard_map.64), channel_id=1, replica_groups=mesh['row'=8,'col'=4] {'row'}, dimensions={0} | all-to-all | bytes 655360 | tf_op jit(solution)/shard_map/all_to_all | solution.py:250
  20.2 4.5 %shard_map.65 = (f32[40,128]{1,0:T(8,128)}, bf16[512,128]{1,0:T(8,128)(2,1)}, f32[8,128]{1,0:T(8,128)}) custom-call(bf16[8,160,128]{2,1,0:T(8,128)(2,1)} %all_to_all.5.buffer_ref.refs_6_, s32[16,128]{1,0:T(8,128)} %bitcast.3, s32[16,128]{1,0:T(8,128)} %bitcast.7), custom_call_target="tpu_custom_call" | custom-call | tf_op jit(solution)/shard_map/pallas_call | solution.py:251
  24.7 1.5 %collective-permute-start.1 = (f32[40,128]{1,0:T(8,128)}, f32[40,128]{1,0:T(8,128)S(1)}, u32[]{:S(2)}, u32[]{:S(2)}) collective-permute-start(f32[40,128]{1,0:T(8,128)} %get-tuple-element.8.refs_0_), channel_id=1, source_target_pairs={{0,2},{1,3},{2,0},{3,1},{4,6},{5,7},{6,4},{7,5},{8,10},{9,11},{10,... | collective-permute-start | bytes 61448 | tf_op jit(solution)/shard_map/ppermute | solution.py:235
  26.2 0.0 collective-permute-start
  26.2 2.5 %collective-permute-done.1.refs_2_ = f32[40,128]{1,0:T(8,128)S(1)} collective-permute-done((f32[40,128]{1,0:T(8,128)}, f32[40,128]{1,0:T(8,128)S(1)}, u32[]{:S(2)}, u32[]{:S(2)}) %collective-permute-start.1) | collective-permute-done | bytes 20512 | tf_op jit(solution)/shard_map/ppermute | solution.py:235
  28.7 0.0 copy-start.1
  28.7 0.0 collective-permute-start.2
  28.7 2.4 %shard_map.66.refs_4_ = f32[256,512]{1,0:T(8,128)} custom-call(s32[2,4]{1,0:T(2,128)} %tiles_ref.3, bf16[256,512]{1,0:T(8,128)(2,1)} %links_ref.3, bf16[8,160,128]{2,1,0:T(8,128)(2,1)} %all_to_all.5.buffer_ref.refs_6_, s32[16,128]{1,0:T(8,128)} %bitcast.4, f32[8,128]{1,0:T(8,128)} %get-tuple-element.9.aux_ref), custom_call_target="tpu_custom_call" | custom-call | flops 1000000 | bytes 1000000 | tf_op jit(solution)/shard_map/pallas_call | solution.py:266
  31.1 0.0 copy-done.1
  31.1 0.0 collective-permute-done.refs_1_
  31.1 0.0 copy-start.2
  31.1 0.0 collective-permute-done.2.refs_3_
  31.1 0.0 copy-start.3
  31.1 0.6 %copy-done.2 = f32[40,128]{1,0:T(8,128)} copy-done((f32[40,128]{1,0:T(8,128)}, f32[40,128]{1,0:T(8,128)S(1)}, u32[]{:S(2)}) %copy-start.2) | copy-done | bytes 20504
  31.7 0.0 copy-done.3
  31.7 3.0 %shard_map.67 = f32[256,128]{1,0:T(8,128)} custom-call(f32[40,128]{1,0:T(8,128)} %get-tuple-element.8.refs_0_, f32[40,128]{1,0:T(8,128)} %copy-done.2, f32[40,128]{1,0:T(8,128)} %copy-done.1, f32[40,128]{1,0:T(8,128)} %copy-done.3, f32[256,512]{1,0:T(8,128)} %shard_map.66.refs_4_, bf16[512,128]{1,0:T(8,128)(2,1)} %get-tuple-element.10.refs_5_, ...), custom_call_target="tpu_custom_call" | custom-call | tf_op jit(solution)/shard_map/pallas_call | solution.py:273
  34.7 0.0 copy-start
  34.7 0.9 %slice.17 = f32[128,128]{1,0:T(8,128)S(1)} slice(f32[256,128]{1,0:T(8,128)} %shard_map.67), slice={[128:256], [0:128]} | slice | bytes 131072 | tf_op jit(solution)/shard_map/slice | solution.py:283
  35.6 0.1 collective-permute-start.3
  35.7 1.1 %collective-permute-done.3 = f32[128,128]{1,0:T(8,128)S(1)} collective-permute-done((f32[128,128]{1,0:T(8,128)S(1)}, f32[128,128]{1,0:T(8,128)S(1)}, u32[]{:S(2)}, u32[]{:S(2)}) %collective-permute-start.3) | collective-permute-done | bytes 65568 | tf_op jit(solution)/shard_map/ppermute | solution.py:235
  36.9 0.0 copy-done
  36.9 1.4 %collective-permute-start.4 = (f32[64,128]{1,0:T(8,128)S(1)}, f32[64,128]{1,0:T(8,128)S(1)}, u32[]{:S(2)}, u32[]{:S(2)}) collective-permute-start(f32[64,128]{1,0:T(8,128)S(1)} %slice.19), channel_id=1, source_target_pairs={{0,2},{1,3},{2,0},{3,1},{4,6},{5,7},{6,4},{7,5},{8,10},{9,11},{10,... | collective-permute-start | bytes 98312 | tf_op jit(solution)/shard_map/ppermute | solution.py:235
  38.3 2.6 %collective-permute-done.4 = f32[64,128]{1,0:T(8,128)S(1)} collective-permute-done((f32[64,128]{1,0:T(8,128)S(1)}, f32[64,128]{1,0:T(8,128)S(1)}, u32[]{:S(2)}, u32[]{:S(2)}) %collective-permute-start.4) | collective-permute-done | bytes 32800 | tf_op jit(solution)/shard_map/ppermute | solution.py:235
  40.9 0.6 %slice_add_fusion.1 = f32[64,128]{1,0:T(8,128)} fusion(f32[64,128]{1,0:T(8,128)S(1)} %collective-permute-done.4, f32[128,128]{1,0:T(8,128)S(1)} %slice_add_fusion), kind=kLoop, calls=%fused_computation.1 | loop fusion | flops 8192 | bytes 98304 | tf_op jit(solution)/shard_map/add | solution.py:283
  (2 shorter events, 0.0 us)
Async XLA Ops:
  24.7 4.0 %collective-permute-start.1 = (f32[40,128]{1,0:T(8,128)}, f32[40,128]{1,0:T(8,128)S(1)}, u32[]{:S(2)}, u32[]{:S(2)}) collective-permute-start(f32[40,128]{1,0:T(8,128)} %get-tuple-element.8.refs_0_), channel_id=1, source_target_pairs={{0,2},{1,3},{2,0},{3,1},{4,6},{5,7},{6,4},{7,5},{8,10},{9,11},{10,... | collective-permute-start | bytes 61448 | tf_op jit(solution)/shard_map/ppermute | solution.py:235
  26.2 4.9 %collective-permute-start = (f32[40,128]{1,0:T(8,128)}, f32[40,128]{1,0:T(8,128)S(1)}, u32[]{:S(2)}, u32[]{:S(2)}) collective-permute-start(f32[40,128]{1,0:T(8,128)} %get-tuple-element.8.refs_0_), channel_id=1, source_target_pairs={{0,1},{1,0},{2,3},{3,2},{4,5},{5,4},{6,7},{7,6},{8,9},{9,8},{10,11... | collective-permute-start | bytes 61448 | tf_op jit(solution)/shard_map/ppermute | solution.py:235
  28.7 2.4 %copy-start.1 = (f32[40,128]{1,0:T(8,128)}, f32[40,128]{1,0:T(8,128)S(1)}, u32[]{:S(2)}) copy-start(f32[40,128]{1,0:T(8,128)S(1)} %collective-permute-done.1.refs_2_) | copy-start | bytes 61444
  28.7 2.4 %collective-permute-start.2 = (f32[40,128]{1,0:T(8,128)S(1)}, f32[40,128]{1,0:T(8,128)S(1)}, u32[]{:S(2)}, u32[]{:S(2)}) collective-permute-start(f32[40,128]{1,0:T(8,128)S(1)} %collective-permute-done.1.refs_2_), channel_id=1, source_target_pairs={{0,1},{1,0},{2,3},{3,2},{4,5},{5,4},{6,7},{7,6},{8,9},{9,8},{10,11... | collective-permute-start | bytes 61448 | tf_op jit(solution)/shard_map/ppermute | solution.py:235
  31.1 0.6 %copy-start.2 = (f32[40,128]{1,0:T(8,128)}, f32[40,128]{1,0:T(8,128)S(1)}, u32[]{:S(2)}) copy-start(f32[40,128]{1,0:T(8,128)S(1)} %collective-permute-done.refs_1_) | copy-start | bytes 61444
  31.1 0.6 %copy-start.3 = (f32[40,128]{1,0:T(8,128)}, f32[40,128]{1,0:T(8,128)S(1)}, u32[]{:S(2)}) copy-start(f32[40,128]{1,0:T(8,128)S(1)} %collective-permute-done.2.refs_3_) | copy-start | bytes 61444
  34.7 2.2 %copy-start = (f32[256,128]{1,0:T(8,128)S(1)}, f32[256,128]{1,0:T(8,128)}, u32[]{:S(2)}) copy-start(f32[256,128]{1,0:T(8,128)} %shard_map.67) | copy-start | bytes 393220
  35.6 1.3 %collective-permute-start.3 = (f32[128,128]{1,0:T(8,128)S(1)}, f32[128,128]{1,0:T(8,128)S(1)}, u32[]{:S(2)}, u32[]{:S(2)}) collective-permute-start(f32[128,128]{1,0:T(8,128)S(1)} %slice.17), channel_id=1, source_target_pairs={{0,1},{1,0},{2,3},{3,2},{4,5},{5,4},{6,7},{7,6},{8,9},{9,8},{10,11... | collective-permute-start | bytes 196616 | tf_op jit(solution)/shard_map/ppermute | solution.py:235
  36.9 4.0 %collective-permute-start.4 = (f32[64,128]{1,0:T(8,128)S(1)}, f32[64,128]{1,0:T(8,128)S(1)}, u32[]{:S(2)}, u32[]{:S(2)}) collective-permute-start(f32[64,128]{1,0:T(8,128)S(1)} %slice.19), channel_id=1, source_target_pairs={{0,2},{1,3},{2,0},{3,1},{4,6},{5,7},{6,4},{7,5},{8,10},{9,11},{10,... | collective-permute-start | bytes 98312 | tf_op jit(solution)/shard_map/ppermute | solution.py:235

commit v2 on v1

v2 whole, which is shorter than its diff:
```python
import functools

import jax
import jax.numpy as jnp
from jax import lax
from jax.experimental import pallas as pl
from jax.experimental.pallas import tpu as pltpu
from jax.sharding import PartitionSpec as P


HOSTS_PIECE = 4
LOCAL_ITERS = 2
HOST_ITERS = 3
LANES = 128
GRANT = 24 * 2**20

damping = 0.85
f32 = jnp.float32
bf16 = jnp.bfloat16

VMEM = pl.BlockSpec(memory_space=pltpu.VMEM)
SMEM = pl.BlockSpec(memory_space=pltpu.SMEM)
HBM = pl.BlockSpec(memory_space=pltpu.HBM)


def iota(shape, axis):
    return lax.broadcasted_iota(jnp.int32, shape, axis)


def mm(a, b):
    return jnp.dot(a, b, preferred_element_type=f32)


def mm_nt(a, b):
    return lax.dot_general(a, b, (((1,), (1,)), ((), ())), preferred_element_type=f32)


def mm_tn(a, b):
    return lax.dot_general(a, b, (((0,), (0,)), ((), ())), preferred_element_type=f32)


def split(x):
    high = x.astype(bf16)
    return high, (x - high.astype(f32)).astype(bf16)


def members(hosts_row, first, count):
    return hosts_row == first + iota((count, hosts_row.shape[1]), 0)


class Sizes:
    def __init__(self, rows, cols, links, tiles, local_links, teleport, pages):
        self.rows, self.cols, self.pages = rows, cols, pages
        self.height, self.width = links
        self.piece = local_links[0]
        self.topics = teleport[1]
        self.tile = self.height // tiles[0]
        self.tile_rows, self.units = tiles
        self.pair = self.tile // self.piece
        self.unit_hosts = self.pair * HOSTS_PIECE
        self.hosts = HOSTS_PIECE * rows * cols
        self.column_hosts = HOSTS_PIECE * rows
        self.row_hosts = HOSTS_PIECE * cols
        self.packed = self.piece * self.piece // LANES
        self.at_counts = self.piece
        self.at_extra = self.at_counts + self.units * self.row_hosts
        self.payload = self.at_extra + 8
        self.extra = (self.units + 1 + 7) // 8 * 8


def rows_of(row, half, piece):
    rolled = pltpu.roll(row, piece, 1)
    low = iota(row.shape, 1) < piece
    first = jnp.where(low, row, rolled)
    second = jnp.where(low, rolled, row)
    return jnp.where(half == 0, first, second)


def first_kernel(s, tiles_hbm, links_hbm, hosts_hbm, dangling_hbm, local_hbm, teleport_hbm, *refs):
    sent_ref, own_ref, chunk_refs = refs[0], refs[1], refs[2 : 2 + s.cols]
    tiles_ref, links_ref, hosts_ref, dangling_ref, local_ref, teleport_ref, sem = refs[2 + s.cols :]
    copies = [
        pltpu.make_async_copy(source, target, sem.at[i])
        for i, (source, target) in enumerate(
            (
                (hosts_hbm, hosts_ref),
                (dangling_hbm, dangling_ref),
                (local_hbm, local_ref),
                (teleport_hbm, teleport_ref),
                (links_hbm, links_ref),
                (tiles_hbm, tiles_ref),
            )
        )
    ]
    for copy in copies:
        copy.start()
    row, column = lax.axis_index("row"), lax.axis_index("col")
    for copy in copies[:4]:
        copy.wait()
    piece = column * s.rows + row
    unit, half = piece // s.pair, piece % s.pair
    hosts = rows_of(hosts_ref[pl.ds(unit, 1), :], half, s.piece)[:, : s.piece]
    keep = rows_of(dangling_ref[pl.ds(unit, 1), :], half, s.piece)[:, : s.piece] == 0
    member = members(hosts, piece * HOSTS_PIECE, 8).astype(bf16)
    same = mm_tn(member, member)
    sameb = same.astype(bf16)
    local = local_ref[...].astype(f32)
    inside = local * same * keep.astype(f32)
    inward = jnp.sum(inside, axis=0, keepdims=True)
    size = jnp.sum(same, axis=0, keepdims=True)
    live = inward > 0
    step = inside * jnp.where(live, 1.0 / jnp.where(live, inward, 1.0), 0.0)
    step = step + same * jnp.where(live, 0.0, 1.0 / size)
    high, low = split(step)
    teleport = teleport_ref[...]
    tele_high, tele_low = split(teleport)
    sizes = jnp.sum(same, axis=1, keepdims=True)
    restart = sizes * teleport / (mm(sameb, tele_high) + mm(sameb, tele_low))
    ranks = damping * jnp.sum(step, axis=1, keepdims=True) + (1 - damping) * restart
    for _ in range(LOCAL_ITERS - 1):
        ranks_high, ranks_low = split(ranks)
        flow = mm(high, ranks_high) + mm(high, ranks_low) + mm(low, ranks_high)
        ranks = damping * flow + (1 - damping) * restart
    half_piece = s.piece // 2
    packed = jnp.concatenate([local[:half_piece], local[half_piece:]], axis=1).astype(bf16)
    own_ref[: s.piece, :] = tele_high
    own_ref[s.piece :, :] = packed
    total = jnp.sum(teleport, axis=0, keepdims=True)
    total_high = total.astype(bf16).astype(f32)
    where = iota((8, LANES), 0)
    inward = jnp.concatenate([inward, inward], axis=1)
    extra = jnp.where(where == 0, inward, jnp.where(where == 1, total_high, total - total_high))

    for copy in copies[4:]:
        copy.wait()
    counts = [[] for _ in range(s.units)]
    for a in range(s.tile_rows):
        tile_row = row * s.tile_rows + a
        first = tile_row * s.unit_hosts
        member = members(hosts_ref[pl.ds(tile_row, 1), :], first, s.unit_hosts)
        sums = mm(member.astype(bf16), links_ref[a * s.tile : (a + 1) * s.tile, :])
        for b in range(s.units):
            unit = column * s.units + b
            target = hosts_ref[pl.ds(unit, 1), :]
            valid = ~members(target, first, s.unit_hosts) & (dangling_ref[pl.ds(unit, 1), :] == 0)
            stored = (tiles_ref[a, b] > 0).astype(f32)
            part = sums[:, b * s.tile : (b + 1) * s.tile]
            counts[b].append(jnp.where(valid, part, 0.0) * stored)
    for k in range(s.cols):
        chunk = column ^ k
        at = pl.multiple_of(chunk * s.piece, s.piece)
        for b in range(s.units):
            lanes = slice(b * s.tile, (b + 1) * s.tile)
            stored = (tiles_ref[chunk // s.pair, b] > 0).astype(f32).astype(bf16)
            chunk_refs[k][:, lanes] = links_ref[pl.ds(at, s.piece), lanes] * stored
    values = jnp.concatenate(
        [ranks.astype(bf16)]
        + [jnp.concatenate(c, axis=0).astype(bf16) for c in counts]
        + [extra.astype(bf16)],
        axis=0,
    )
    for n in range(s.rows):
        sent_ref[n] = values


def graph_kernel(s, buffer_ref, hosts_ref, shared_ref, local_ref):
    column = lax.axis_index("col")
    ones = jnp.ones((8, LANES), bf16)
    low = iota((1, LANES), 1) < s.piece
    extras = [buffer_ref[n, s.at_extra :, :].astype(f32) for n in range(s.rows)]
    total = functools.reduce(jnp.add, [e[1:2] + e[2:3] for e in extras])
    for m in range(s.units):
        unit = column * s.units + m
        member = members(hosts_ref[pl.ds(unit, 1), :], unit * s.unit_hosts, s.unit_hosts)
        start = s.at_counts + m * s.row_hosts
        counts = jnp.concatenate(
            [buffer_ref[n, start : start + s.row_hosts, :] for n in range(s.rows)], axis=0
        )
        ranks = jnp.concatenate(
            [buffer_ref[s.pair * m + q, : s.piece, :] for q in range(s.pair)], axis=0
        )
        local_ref[m * s.tile : (m + 1) * s.tile, :] = ranks
        inward = jnp.where(low, extras[s.pair * m][:1], extras[s.pair * m + 1][:1])
        degree = inward + mm(jnp.ones((8, s.hosts), bf16), counts)[:1]
        has_out = degree > 0
        inverse = jnp.where(has_out, 1.0 / jnp.where(has_out, degree, 1.0), 0.0)
        means = mm_nt(ones[:, : s.topics], ranks)[:1] * (1.0 / s.topics) * inverse
        weights = mm_nt((member.astype(f32) * means).astype(bf16), counts)
        out = jnp.sum(weights, axis=1, keepdims=True)
        linked = out > 0
        norm = jnp.where(linked, weights / jnp.where(linked, out, 1.0), 1.0 / s.hosts)
        shared_ref[m * s.unit_hosts : (m + 1) * s.unit_hosts, :] = norm
        shared_ref[s.column_hosts + m : s.column_hosts + m + 1, :LANES] = inverse
    shared_ref[s.column_hosts + s.units : s.column_hosts + s.units + 1, : s.topics] = total


def edges_kernel(s, own_ref, hosts_ref, dangling_ref, *refs):
    chunk_refs, out_ref = refs[: s.cols], refs[s.cols]
    row, column = lax.axis_index("row"), lax.axis_index("col")
    for k in range(s.cols):
        at = pl.multiple_of((column ^ k) * s.width, s.width)
        out_ref[:, pl.ds(at, s.width)] = chunk_refs[k][...]
    piece = row * s.cols + column
    unit, half = piece // s.pair, piece % s.pair
    hosts = hosts_ref[pl.ds(unit, 1), :]
    keep = dangling_ref[pl.ds(unit, 1), :] == 0
    mine = rows_of(hosts, half, s.piece)[:, : s.piece]
    first = piece * HOSTS_PIECE
    same = mm_tn(members(mine, first, 8).astype(bf16), members(hosts, first, 8).astype(bf16)) > 0
    packed = own_ref[s.piece :, :].astype(f32)
    rolled = pltpu.roll(packed, s.piece, 1)
    low = iota((s.packed, LANES), 1) < s.piece
    local = jnp.concatenate([jnp.where(low, packed, rolled), jnp.where(low, rolled, packed)], axis=0)
    at = pl.multiple_of(unit * s.tile, s.tile)
    across = out_ref[:, pl.ds(at, s.tile)].astype(f32)
    fixed = jnp.where(same, jnp.where(keep, local, 0.0), across)
    out_ref[:, pl.ds(at, s.tile)] = fixed.astype(bf16)


def three(x):
    high = x.astype(bf16).astype(f32)
    rest = x - high
    middle = rest.astype(bf16).astype(f32)
    where = iota((8, x.shape[1]), 0)
    parts = jnp.where(where == 0, high, jnp.where(where == 1, middle, rest - middle))
    return jnp.where(where < 3, parts, 0.0).astype(bf16)


def host_kernel(s, own_ref, hosts_ref, edges_ref, *refs):
    shared, (weighted_ref, base_ref, full_ref, inverse_ref) = refs[: s.cols], refs[s.cols :]
    column = lax.axis_index("col")
    total = jnp.zeros((1, s.topics), f32)
    for k in range(s.cols):
        at = pl.multiple_of((column ^ k) * s.column_hosts, s.column_hosts)
        full_ref[pl.ds(at, s.column_hosts), :] = shared[k][: s.column_hosts, :]
        end = s.column_hosts + s.units
        inverse_ref[pl.ds((column ^ k) * s.units, s.units), :] = shared[k][s.column_hosts : end, :LANES]
        total = total + shared[k][end : end + 1, : s.topics]
    base_ref[...] = (1 - damping) * s.pages * own_ref[: s.piece, :].astype(f32) / total
    norm = full_ref[...]
    norm_high, norm_low = split(norm)
    rank = damping * jnp.sum(norm, axis=0, keepdims=True) + (1 - damping)
    for _ in range(HOST_ITERS - 1):
        parts = three(rank)
        fresh = mm(parts, norm_high) + mm(parts, norm_low)
        rank = damping * jnp.sum(fresh, axis=0, keepdims=True) + (1 - damping)
    block = LANES // s.unit_hosts
    all_units = s.units * s.cols
    for g in range(s.hosts // LANES):
        count = min(block, all_units - g * block)
        hosts = hosts_ref[g * block : g * block + count, :] - g * LANES
        ranks = jnp.broadcast_to(rank[:, g * LANES : (g + 1) * LANES], (count, LANES))
        page = damping * jnp.take_along_axis(ranks, hosts, axis=1)
        inverse = inverse_ref[g * block : g * block + count, :]
        scale = page * inverse
        dead = jnp.where(inverse > 0, 0.0, page * (1.0 / s.pages))
        for u in range(count):
            at = (g * block + u) * s.tile
            lanes = slice(at, at + s.tile)
            links = edges_ref[:, lanes].astype(f32)
            weighted_ref[:, lanes] = (links * scale[u : u + 1] + dead[u : u + 1]).astype(bf16)


def flow_kernel(s, weighted_ref, base_ref, *refs):
    locals_, out_ref = refs[: s.cols], refs[s.cols]
    column = lax.axis_index("col")
    flow = base_ref[...]
    for k in range(s.cols):
        at = pl.multiple_of((column ^ k) * s.width, s.width)
        flow = flow + mm(weighted_ref[:, pl.ds(at, s.width)], locals_[k][...])
    out_ref[...] = flow


def in_hbm(x):
    return pltpu.with_memory_space_constraint(x, pltpu.HBM)


def swap(x, count, bits):
    return lax.ppermute(x, "col", [(i, i ^ bits) for i in range(count)])


def gathered(x, count):
    found = {0: x}
    bit = count // 2
    while bit:
        for k, v in list(found.items()):
            found[k ^ bit] = swap(v, count, bit)
        bit //= 2
    return [found[k] for k in range(count)]


def call(kernel, out_shape, in_specs, scratch=(), cost=10**6):
    single = not isinstance(out_shape, tuple)
    return pl.pallas_call(
        kernel,
        out_shape=out_shape,
        in_specs=in_specs,
        out_specs=VMEM if single else (VMEM,) * len(out_shape),
        scratch_shapes=scratch,
        compiler_params=pltpu.CompilerParams(vmem_limit_bytes=GRANT),
        cost_estimate=pl.CostEstimate(flops=cost, bytes_accessed=cost, transcendentals=0),
    )


def on_device(links, tiles, local_links, host_ids, dangling, teleport):
    rows, cols = lax.axis_size("row"), lax.axis_size("col")
    pages = host_ids.shape[0]
    s = Sizes(rows, cols, links.shape, tiles.shape, local_links.shape, teleport.shape, pages)
    hosts = host_ids.reshape(pages // LANES, LANES)
    ignored = dangling.reshape(pages // LANES, LANES)
    shape = jax.ShapeDtypeStruct
    sent, own, *chunks = call(
        functools.partial(first_kernel, s),
        (
            shape((rows, s.payload, LANES), bf16),
            shape((s.piece + s.packed, LANES), bf16),
            *(shape((s.piece, s.width), bf16) for _ in range(cols)),
        ),
        [HBM] * 6,
        [pltpu.SMEM(tiles.shape, tiles.dtype)]
        + [pltpu.VMEM(a.shape, a.dtype) for a in (links, hosts, ignored, local_links, teleport)]
        + [pltpu.SemaphoreType.DMA((6,))],
    )(*(in_hbm(x) for x in (tiles, links, hosts, ignored, local_links, teleport)))
    moves = [(r * cols + c, c * rows + r) for r in range(rows) for c in range(cols)]
    own = lax.ppermute(own, ("row", "col"), moves)
    for k in range(1, cols):
        chunks[k] = swap(chunks[k], cols, k)
    held = lax.all_to_all(sent, "row", 0, 0, tiled=True)
    shared, local = call(
        functools.partial(graph_kernel, s),
        (
            shape((s.column_hosts + s.extra, s.hosts), f32),
            shape((s.width, s.topics), bf16),
        ),
        [VMEM] * 2,
    )(held, hosts)
    shared = gathered(shared, cols)
    locals_ = gathered(local, cols)
    edges = call(
        functools.partial(edges_kernel, s),
        shape((s.piece, pages), bf16),
        [VMEM] * (3 + cols),
    )(own, hosts, ignored, *chunks)
    weighted, base = call(
        functools.partial(host_kernel, s),
        (shape((s.piece, pages), bf16), shape((s.piece, s.topics), f32)),
        [VMEM] * (3 + cols),
        [pltpu.VMEM((s.hosts, s.hosts), f32), pltpu.VMEM((s.units * cols, LANES), f32)],
    )(own, hosts, edges, *shared)
    return call(
        functools.partial(flow_kernel, s),
        shape((s.piece, s.topics), f32),
        [VMEM] * (2 + cols),
    )(weighted, base, *locals_)


def solution(mesh):
    return jax.shard_map(
        on_device,
        mesh=mesh,
        in_specs=(
            P("row", "col"),
            P("row", "col"),
            P(("col", "row"), None),
            P(),
            P(),
            P(("col", "row"), None),
        ),
        out_specs=P(("row", "col"), None),
        check_vma=False,
    )
```

time: 41.8 us -> 39.7 us (0.950)
  Pallas kernels: 11.8 us -> 3.95 us
  starting transfers between devices: 3.03 us -> 10.7 us
  local copies, waits for them, and re-layouts: 1.52 us -> 0.01 us
  waiting for transfers between devices: 6.2 us -> 7.63 us
  blocking collectives: 18.3 us -> 17.1 us
  other arithmetic: 0.63 us -> 0 us
    pallas_call x4 -> x5, Pallas kernels: 11.8 us -> 3.95 us  [the longest x1 1.58 us: on_device(): call(functools.partial(first_kernel, s), (shape((rows, s.payload, LANES),...]
    ppermute x5 -> x10, starting transfers between devices: 3.03 us -> 10.7 us  [the longest x9 10 us: swap(): return lax.ppermute(x, 'col', [(i, i ^ bits) for i in range(count)])]
    ppermute x5 -> x10, waiting for transfers between devices: 6.2 us -> 7.63 us  [the longest x9 7.63 us: swap(): return lax.ppermute(x, 'col', [(i, i ^ bits) for i in range(count)])]
    all_to_all x1, blocking collectives: 18.3 us -> 17.1 us  [on_device(): held = lax.all_to_all(sent, 'row', 0, 0, tiled=True)]
    slice x2 -> x0, local copies, waits for them, and re-layouts: 0.92 us -> none  [on_device(): flows = flows[:half] + swap(flows[half:], cols, bit)]
    add x2 -> x0, other arithmetic: 0.63 us -> none  [on_device(): flows = flows[:half] + swap(flows[half:], cols, bit)]
    unnamed x8 -> x4, local copies, waits for them, and re-layouts: 0.6 us -> 0.01 us
  transfers between devices with their start and end apart: 5 -> 10, of which waited for: 3 -> 3; matrix products, arithmetic and copies ran while one was open for 0% -> 0% of each run, Pallas kernels for 6% -> 2%
where the time goes in v2:
time: 39.7 us; the launch traced here: 39.4 us
  blocking collectives  17.1 us (43%)
  starting transfers between devices  10.7 us (27%)
  waiting for transfers between devices  7.63 us (19%)
  Pallas kernels  3.95 us (10%)
    all_to_all x1, blocking collectives, on_device(): held = lax.all_to_all(sent, 'row', 0, 0, tiled=True)  17.1 us
    ppermute x9, starting transfers between devices, swap(): return lax.ppermute(x, 'col', [(i, i ^ bits) for i in range(count)])  10 us
    ppermute x9, waiting for transfers between devices, swap(): return lax.ppermute(x, 'col', [(i, i ^ bits) for i in range(count)])  7.63 us
    pallas_call x1, Pallas kernels, on_device(): call(functools.partial(first_kernel, s), (shape((rows, s.payload, LANES),...  1.58 us
    pallas_call x1, Pallas kernels, on_device(): call(functools.partial(flow_kernel, s), shape((s.piece, s.topics), f32),...  0.84 us
  transfers between devices with their start and end apart: 10, of which 3 were waited for; matrix products, arithmetic and copies ran while one was open for 0% of the time, Pallas kernels for 2%

profile of v2, /device:TPU:0, one launch (start us, length us, event | category | flops | bytes accessed | tf_op | source)
XLA Modules:
  0.0 39.4 jit_solution(9992628360101092890)
XLA Ops:
  0.0 1.6 %shard_map.64 = (bf16[8,136,128]{2,1,0:T(8,128)(2,1)S(1)}, bf16[96,128]{1,0:T(8,128)(2,1)S(1)}, bf16[64,512]{1,0:T(8,128)(2,1)S(1)}, bf16[64,512]{1,0:T(8,128)(2...) custom-call(s32[2,4]{1,0:T(2,128)} %tiles_hbm.1, bf16[256,512]{1,0:T(8,128)(2,1)} %links_hbm.1, ...), custom_call_target="tpu_custom_call" | custom-call | flops 1000000 | bytes 1000000 | tf_op jit(solution)/shard_map/pallas_call | solution.py:312
  1.6 0.0 copy-start
  1.6 17.1 %all_to_all.5.buffer_ref = bf16[8,136,128]{2,1,0:T(8,128)(2,1)S(1)} all-to-all(bf16[8,136,128]{2,1,0:T(8,128)(2,1)S(1)} %get-tuple-element.20), channel_id=1, replica_groups=mesh['row'=8,'col'=4] {'row'}, dimensions={0} | all-to-all | bytes 557056 | tf_op jit(solution)/shard_map/all_to_all | solution.py:328
  18.7 0.0 copy-done
  18.7 0.8 %shard_map.66 = (f32[40,128]{1,0:T(8,128)S(1)}, bf16[512,128]{1,0:T(8,128)(2,1)S(1)}) custom-call(bf16[8,136,128]{2,1,0:T(8,128)(2,1)S(1)} %all_to_all.5.buffer_ref, s32[16,128]{1,0:T(8,128)S(1)} %bitcast.3), custom_call_target="tpu_custom_call" | custom-call | flops 1000000 | bytes 1000000 | tf_op jit(solution)/shard_map/pallas_call | solution.py:329
  19.5 0.0 copy-start.1
  19.5 1.6 %collective-permute-start.8 = (bf16[512,128]{1,0:T(8,128)(2,1)S(1)}, bf16[512,128]{1,0:T(8,128)(2,1)S(1)}, u32[]{:S(2)}, u32[]{:S(2)}) collective-permute-start(bf16[512,128]{1,0:T(8,128)(2,1)S(1)} %get-tuple-element.24.refs_0_), channel_id=1, source_target_pairs={{0,2},{1,3},{2,0},{3,1},{4,6},{5,7},{6,4},{7,5},{8,10},{9,11},{10,... | collective-permute-start | bytes 393224 | tf_op jit(solution)/shard_map/ppermute | solution.py:279
  21.1 0.0 collective-permute-start.7
  21.1 3.4 %collective-permute-done.8.refs_2_ = bf16[512,128]{1,0:T(8,128)(2,1)S(1)} collective-permute-done((bf16[512,128]{1,0:T(8,128)(2,1)S(1)}, bf16[512,128]{1,0:T(8,128)(2,1)S(1)}, u32[]{:S(2)}, u32[]{:S(2)}) %collective-permute-start.8) | collective-permute-done | bytes 131104 | tf_op jit(solution)/shard_map/ppermute | solution.py:279
  24.5 0.0 collective-permute-start.9
  24.5 0.5 %collective-permute-start.1 = (bf16[64,512]{1,0:T(8,128)(2,1)S(1)}, bf16[64,512]{1,0:T(8,128)(2,1)S(1)}, u32[]{:S(2)}, u32[]{:S(2)}) collective-permute-start(bf16[64,512]{1,0:T(8,128)(2,1)S(1)} %get-tuple-element.17), channel_id=1, source_target_pairs={{0,1},{1,0},{2,3},{3,2},{4,5},{5,4},{6,7},{7,6},{8,9},{9,8},{10,11... | collective-permute-start | bytes 196616 | tf_op jit(solution)/shard_map/ppermute | solution.py:279
  25.0 0.7 %collective-permute-start = (bf16[96,128]{1,0:T(8,128)(2,1)S(1)}, bf16[96,128]{1,0:T(8,128)(2,1)S(1)}, u32[]{:S(2)}, u32[]{:S(2)}) collective-permute-start(bf16[96,128]{1,0:T(8,128)(2,1)S(1)} %get-tuple-element.15), channel_id=1, source_target_pairs={{0,0},{1,8},{2,16},{3,24},{4,1},{5,9},{6,17},{7,25},{8,2},{9,10},{... | collective-permute-start | bytes 73736 | tf_op jit(solution)/shard_map/ppermute | solution.py:325
  25.7 3.5 %collective-permute-start.2 = (bf16[64,512]{1,0:T(8,128)(2,1)S(1)}, bf16[64,512]{1,0:T(8,128)(2,1)S(1)}, u32[]{:S(2)}, u32[]{:S(2)}) collective-permute-start(bf16[64,512]{1,0:T(8,128)(2,1)S(1)} %get-tuple-element.18), channel_id=1, source_target_pairs={{0,2},{1,3},{2,0},{3,1},{4,6},{5,7},{6,4},{7,5},{8,10},{9,11},{10,... | collective-permute-start | bytes 196616 | tf_op jit(solution)/shard_map/ppermute | solution.py:279
  29.2 0.0 collective-permute-done.own_ref
  29.2 4.0 %collective-permute-start.3 = (bf16[64,512]{1,0:T(8,128)(2,1)S(1)}, bf16[64,512]{1,0:T(8,128)(2,1)S(1)}, u32[]{:S(2)}, u32[]{:S(2)}) collective-permute-start(bf16[64,512]{1,0:T(8,128)(2,1)S(1)} %get-tuple-element.19), channel_id=1, source_target_pairs={{0,3},{1,2},{2,1},{3,0},{4,7},{5,6},{6,5},{7,4},{8,11},{9,10},{10,... | collective-permute-start | bytes 196616 | tf_op jit(solution)/shard_map/ppermute | solution.py:279
  33.1 0.0 collective-permute-done.1.refs_1_
  33.1 0.3 collective-permute-start.5
  33.4 0.0 collective-permute-done.2.refs_2_
  33.4 0.2 collective-permute-start.4
  33.6 3.3 %collective-permute-done.5.refs_2_ = f32[40,128]{1,0:T(8,128)S(1)} collective-permute-done((f32[40,128]{1,0:T(8,128)S(1)}, f32[40,128]{1,0:T(8,128)S(1)}, u32[]{:S(2)}, u32[]{:S(2)}) %collective-permute-start.5) | collective-permute-done | bytes 20512 | tf_op jit(solution)/shard_map/ppermute | solution.py:279
  36.9 0.0 collective-permute-start.6
  36.9 0.0 collective-permute-done.3.refs_3_
  36.9 0.0 copy-done.1
  36.9 0.3 shard_map.65.edges_ref
  37.2 0.0 collective-permute-done.4.refs_1_
  37.2 0.9 %collective-permute-done.6.refs_3_ = f32[40,128]{1,0:T(8,128)S(1)} collective-permute-done((f32[40,128]{1,0:T(8,128)S(1)}, f32[40,128]{1,0:T(8,128)S(1)}, u32[]{:S(2)}, u32[]{:S(2)}) %collective-permute-start.6) | collective-permute-done | bytes 20512 | tf_op jit(solution)/shard_map/ppermute | solution.py:279
  38.1 0.5 %shard_map.67 = (bf16[64,2048]{1,0:T(8,128)(2,1)S(1)}, f32[64,128]{1,0:T(8,128)S(1)}) custom-call(bf16[96,128]{1,0:T(8,128)(2,1)S(1)} %collective-permute-done.own_ref, s32[16,128]{1,0:T(8,128)S(1)} %bitcast.5, bf16[64,2048]{1,0:T(8,128)(2,1)S(1)} %shard_map.65.edges_ref, f32[40,128]{1,0:T(8,128)S(1)} %get-tuple-element.21.refs_0_, ...), custom_call_target="tpu_custom_call" | custom-call | flops 1000000 | bytes 1000000 | tf_op jit(solution)/shard_map/pallas_call | solution.py:344
  38.6 0.0 collective-permute-done.7.refs_1_
  38.6 0.0 collective-permute-done.9.refs_3_
  38.6 0.8 %shard_map.68 = f32[64,128]{1,0:T(8,128)} custom-call(bf16[64,2048]{1,0:T(8,128)(2,1)S(1)} %get-tuple-element.22.weighted_ref, f32[64,128]{1,0:T(8,128)S(1)} %get-tuple-element.23.base_ref, bf16[512,128]{1,0:T(8,128)(2,1)S(1)} %get-tuple-element.24.refs_0_, bf16[512,128]{1,0:T(8,128)(2,1)S(1)} %collective-permute-done.7.refs_1_, ...), custom_call_target="tpu_custom_call" | custom-call | flops 1000000 | bytes 1000000 | tf_op jit(solution)/shard_map/pallas_call | solution.py:350
Async XLA Ops:
  1.6 17.1 %copy-start = (s32[2048]{0:T(1024)S(1)}, s32[2048]{0:T(1024)}, u32[]{:S(2)}) copy-start(s32[2048]{0:T(1024)} %param.9) | copy-start | bytes 24580
  19.5 17.4 %copy-start.1 = (s32[2048]{0:T(1024)S(1)}, s32[2048]{0:T(1024)}, u32[]{:S(2)}) copy-start(s32[2048]{0:T(1024)} %param.10) | copy-start | bytes 24580
  19.5 5.0 %collective-permute-start.8 = (bf16[512,128]{1,0:T(8,128)(2,1)S(1)}, bf16[512,128]{1,0:T(8,128)(2,1)S(1)}, u32[]{:S(2)}, u32[]{:S(2)}) collective-permute-start(bf16[512,128]{1,0:T(8,128)(2,1)S(1)} %get-tuple-element.24.refs_0_), channel_id=1, source_target_pairs={{0,2},{1,3},{2,0},{3,1},{4,6},{5,7},{6,4},{7,5},{8,10},{9,11},{10,... | collective-permute-start | bytes 393224 | tf_op jit(solution)/shard_map/ppermute | solution.py:279
  21.1 17.5 %collective-permute-start.7 = (bf16[512,128]{1,0:T(8,128)(2,1)S(1)}, bf16[512,128]{1,0:T(8,128)(2,1)S(1)}, u32[]{:S(2)}, u32[]{:S(2)}) collective-permute-start(bf16[512,128]{1,0:T(8,128)(2,1)S(1)} %get-tuple-element.24.refs_0_), channel_id=1, source_target_pairs={{0,1},{1,0},{2,3},{3,2},{4,5},{5,4},{6,7},{7,6},{8,9},{9,8},{10,11... | collective-permute-start | bytes 393224 | tf_op jit(solution)/shard_map/ppermute | solution.py:279
  24.5 14.1 %collective-permute-start.9 = (bf16[512,128]{1,0:T(8,128)(2,1)S(1)}, bf16[512,128]{1,0:T(8,128)(2,1)S(1)}, u32[]{:S(2)}, u32[]{:S(2)}) collective-permute-start(bf16[512,128]{1,0:T(8,128)(2,1)S(1)} %collective-permute-done.8.refs_2_), channel_id=1, source_target_pairs={{0,1},{1,0},{2,3},{3,2},{4,5},{5,4},{6,7},{7,6},{8,9},{9,8},{10,11... | collective-permute-start | bytes 393224 | tf_op jit(solution)/shard_map/ppermute | solution.py:279
  24.5 8.6 %collective-permute-start.1 = (bf16[64,512]{1,0:T(8,128)(2,1)S(1)}, bf16[64,512]{1,0:T(8,128)(2,1)S(1)}, u32[]{:S(2)}, u32[]{:S(2)}) collective-permute-start(bf16[64,512]{1,0:T(8,128)(2,1)S(1)} %get-tuple-element.17), channel_id=1, source_target_pairs={{0,1},{1,0},{2,3},{3,2},{4,5},{5,4},{6,7},{7,6},{8,9},{9,8},{10,11... | collective-permute-start | bytes 196616 | tf_op jit(solution)/shard_map/ppermute | solution.py:279
  25.0 4.1 %collective-permute-start = (bf16[96,128]{1,0:T(8,128)(2,1)S(1)}, bf16[96,128]{1,0:T(8,128)(2,1)S(1)}, u32[]{:S(2)}, u32[]{:S(2)}) collective-permute-start(bf16[96,128]{1,0:T(8,128)(2,1)S(1)} %get-tuple-element.15), channel_id=1, source_target_pairs={{0,0},{1,8},{2,16},{3,24},{4,1},{5,9},{6,17},{7,25},{8,2},{9,10},{... | collective-permute-start | bytes 73736 | tf_op jit(solution)/shard_map/ppermute | solution.py:325
  25.7 7.8 %collective-permute-start.2 = (bf16[64,512]{1,0:T(8,128)(2,1)S(1)}, bf16[64,512]{1,0:T(8,128)(2,1)S(1)}, u32[]{:S(2)}, u32[]{:S(2)}) collective-permute-start(bf16[64,512]{1,0:T(8,128)(2,1)S(1)} %get-tuple-element.18), channel_id=1, source_target_pairs={{0,2},{1,3},{2,0},{3,1},{4,6},{5,7},{6,4},{7,5},{8,10},{9,11},{10,... | collective-permute-start | bytes 196616 | tf_op jit(solution)/shard_map/ppermute | solution.py:279
  29.2 7.7 %collective-permute-start.3 = (bf16[64,512]{1,0:T(8,128)(2,1)S(1)}, bf16[64,512]{1,0:T(8,128)(2,1)S(1)}, u32[]{:S(2)}, u32[]{:S(2)}) collective-permute-start(bf16[64,512]{1,0:T(8,128)(2,1)S(1)} %get-tuple-element.19), channel_id=1, source_target_pairs={{0,3},{1,2},{2,1},{3,0},{4,7},{5,6},{6,5},{7,4},{8,11},{9,10},{10,... | collective-permute-start | bytes 196616 | tf_op jit(solution)/shard_map/ppermute | solution.py:279
  33.1 3.8 %collective-permute-start.5 = (f32[40,128]{1,0:T(8,128)S(1)}, f32[40,128]{1,0:T(8,128)S(1)}, u32[]{:S(2)}, u32[]{:S(2)}) collective-permute-start(f32[40,128]{1,0:T(8,128)S(1)} %get-tuple-element.21.refs_0_), channel_id=1, source_target_pairs={{0,2},{1,3},{2,0},{3,1},{4,6},{5,7},{6,4},{7,5},{8,10},{9,11},{10,... | collective-permute-start | bytes 61448 | tf_op jit(solution)/shard_map/ppermute | solution.py:279
  33.4 3.7 %collective-permute-start.4 = (f32[40,128]{1,0:T(8,128)S(1)}, f32[40,128]{1,0:T(8,128)S(1)}, u32[]{:S(2)}, u32[]{:S(2)}) collective-permute-start(f32[40,128]{1,0:T(8,128)S(1)} %get-tuple-element.21.refs_0_), channel_id=1, source_target_pairs={{0,1},{1,0},{2,3},{3,2},{4,5},{5,4},{6,7},{7,6},{8,9},{9,8},{10,11... | collective-permute-start | bytes 61448 | tf_op jit(solution)/shard_map/ppermute | solution.py:279
  36.9 1.2 %collective-permute-start.6 = (f32[40,128]{1,0:T(8,128)S(1)}, f32[40,128]{1,0:T(8,128)S(1)}, u32[]{:S(2)}, u32[]{:S(2)}) collective-permute-start(f32[40,128]{1,0:T(8,128)S(1)} %collective-permute-done.5.refs_2_), channel_id=1, source_target_pairs={{0,1},{1,0},{2,3},{3,2},{4,5},{5,4},{6,7},{7,6},{8,9},{9,8},{10,11... | collective-permute-start | bytes 61448 | tf_op jit(solution)/shard_map/ppermute | solution.py:279

commit v3 on v2

--- a/solution.py
+++ b/solution.py
@@ -163,7 +163,12 @@
         sent_ref[n] = values
 
 
-def graph_kernel(s, buffer_ref, hosts_ref, shared_ref, local_ref):
+def ranks_kernel(s, buffer_ref, local_ref):
+    for n in range(s.rows):
+        local_ref[n * s.piece : (n + 1) * s.piece, :] = buffer_ref[n, : s.piece, :]
+
+
+def graph_kernel(s, buffer_ref, hosts_ref, local_ref, shared_ref):
     column = lax.axis_index("col")
     ones = jnp.ones((8, LANES), bf16)
     low = iota((1, LANES), 1) < s.piece
@@ -176,10 +181,7 @@
         counts = jnp.concatenate(
             [buffer_ref[n, start : start + s.row_hosts, :] for n in range(s.rows)], axis=0
         )
-        ranks = jnp.concatenate(
-            [buffer_ref[s.pair * m + q, : s.piece, :] for q in range(s.pair)], axis=0
-        )
-        local_ref[m * s.tile : (m + 1) * s.tile, :] = ranks
+        ranks = local_ref[m * s.tile : (m + 1) * s.tile, :]
         inward = jnp.where(low, extras[s.pair * m][:1], extras[s.pair * m + 1][:1])
         degree = inward + mm(jnp.ones((8, s.hosts), bf16), counts)[:1]
         has_out = degree > 0
@@ -261,13 +263,13 @@
             weighted_ref[:, lanes] = (links * scale[u : u + 1] + dead[u : u + 1]).astype(bf16)
 
 
-def flow_kernel(s, weighted_ref, base_ref, *refs):
-    locals_, out_ref = refs[: s.cols], refs[s.cols]
+def flow_kernel(s, distances, weighted_ref, base_ref, *refs):
+    locals_, out_ref = refs[:-1], refs[-1]
     column = lax.axis_index("col")
     flow = base_ref[...]
-    for k in range(s.cols):
+    for k, local_ref in zip(distances, locals_, strict=True):
         at = pl.multiple_of((column ^ k) * s.width, s.width)
-        flow = flow + mm(weighted_ref[:, pl.ds(at, s.width)], locals_[k][...])
+        flow = flow + mm(weighted_ref[:, pl.ds(at, s.width)], local_ref[...])
     out_ref[...] = flow
 
 
@@ -287,6 +289,13 @@
             found[k ^ bit] = swap(v, count, bit)
         bit //= 2
     return [found[k] for k in range(count)]
+
+
+def spread(values, count):
+    found = [values[0]]
+    for k in range(1, count):
+        found.append(swap(values[k], count, k))
+    return found
 
 
 def call(kernel, out_shape, in_specs, scratch=(), cost=10**6):
@@ -323,19 +332,16 @@
     )(*(in_hbm(x) for x in (tiles, links, hosts, ignored, local_links, teleport)))
     moves = [(r * cols + c, c * rows + r) for r in range(rows) for c in range(cols)]
     own = lax.ppermute(own, ("row", "col"), moves)
-    for k in range(1, cols):
-        chunks[k] = swap(chunks[k], cols, k)
+    chunks = spread(chunks, cols)
     held = lax.all_to_all(sent, "row", 0, 0, tiled=True)
-    shared, local = call(
+    local = call(functools.partial(ranks_kernel, s), shape((s.width, s.topics), bf16), [VMEM])(held)
+    locals_ = gathered(local, cols)
+    shared = call(
         functools.partial(graph_kernel, s),
-        (
-            shape((s.column_hosts + s.extra, s.hosts), f32),
-            shape((s.width, s.topics), bf16),
-        ),
-        [VMEM] * 2,
-    )(held, hosts)
-    shared = gathered(shared, cols)
-    locals_ = gathered(local, cols)
+        shape((s.column_hosts + s.extra, s.hosts), f32),
+        [VMEM] * 3,
+    )(held, hosts, local)
+    shared = spread([shared] * cols, cols)
     edges = call(
         functools.partial(edges_kernel, s),
         shape((s.piece, pages), bf16),
@@ -347,11 +353,16 @@
         [VMEM] * (3 + cols),
         [pltpu.VMEM((s.hosts, s.hosts), f32), pltpu.VMEM((s.units * cols, LANES), f32)],
     )(own, hosts, edges, *shared)
-    return call(
-        functools.partial(flow_kernel, s),
-        shape((s.piece, s.topics), f32),
-        [VMEM] * (2 + cols),
-    )(weighted, base, *locals_)
+    late = [k for k in range(cols) if k % 2 and k > 1]
+    soon = [k for k in range(cols) if k not in late]
+    flow = base
+    for distances in (soon, late):
+        flow = call(
+            functools.partial(flow_kernel, s, distances),
+            shape((s.piece, s.topics), f32),
+            [VMEM] * (2 + len(distances)),
+        )(weighted, flow, *(locals_[k] for k in distances))
+    return flow
 
 
 def solution(mesh):

time: 39.7 us -> 38.9 us (0.980)
  waiting for transfers between devices: 7.63 us -> 5.46 us
  starting transfers between devices: 10.7 us -> 11.9 us
    ppermute x9, waiting for transfers between devices: 7.63 us -> 5.46 us  [swap(): return lax.ppermute(x, 'col', [(i, i ^ bits) for i in range(count)])]
    ppermute x9, starting transfers between devices: 10 us -> 11.2 us  [swap(): return lax.ppermute(x, 'col', [(i, i ^ bits) for i in range(count)])]
    pallas_call x2 -> x4, Pallas kernels: 1.61 us -> 1.76 us  [the longest x2 0.98 us: on_device(): call(functools.partial(flow_kernel, s, distances), shape((s.piece, s.topi...]
  transfers between devices with their start and end apart: 10 -> 10, of which waited for: 3 -> 4; matrix products, arithmetic and copies ran while one was open for 0% -> 0% of each run, Pallas kernels for 2% -> 4%
where the time goes in v3:
time: 38.9 us; the launch traced here: 38.6 us
  blocking collectives  17.1 us (44%)
  starting transfers between devices  11.9 us (31%)
  waiting for transfers between devices  5.46 us (14%)
  Pallas kernels  4.09 us (11%)
    all_to_all x1, blocking collectives, on_device(): held = lax.all_to_all(sent, 'row', 0, 0, tiled=True)  17.1 us
    ppermute x9, starting transfers between devices, swap(): return lax.ppermute(x, 'col', [(i, i ^ bits) for i in range(count)])  11.2 us
    ppermute x9, waiting for transfers between devices, swap(): return lax.ppermute(x, 'col', [(i, i ^ bits) for i in range(count)])  5.46 us
    pallas_call x1, Pallas kernels, on_device(): call(functools.partial(first_kernel, s), (shape((rows, s.payload, LANES),...  1.58 us
    pallas_call x2, Pallas kernels, on_device(): call(functools.partial(flow_kernel, s, distances), shape((s.piece, s.topi...  0.98 us
  transfers between devices with their start and end apart: 10, of which 4 were waited for; matrix products, arithmetic and copies ran while one was open for 0% of the time, Pallas kernels for 4%

profile of v3, /device:TPU:0, one launch (start us, length us, event | category | flops | bytes accessed | tf_op | source)
XLA Modules:
  0.0 38.6 jit_solution(3686248197587560129)
XLA Ops:
  0.0 1.6 %shard_map.64 = (bf16[8,136,128]{2,1,0:T(8,128)(2,1)S(1)}, bf16[96,128]{1,0:T(8,128)(2,1)S(1)}, bf16[64,512]{1,0:T(8,128)(2,1)S(1)}, bf16[64,512]{1,0:T(8,128)(2...) custom-call(s32[2,4]{1,0:T(2,128)} %tiles_hbm.1, bf16[256,512]{1,0:T(8,128)(2,1)} %links_hbm.1, ...), custom_call_target="tpu_custom_call" | custom-call | flops 1000000 | bytes 1000000 | tf_op jit(solution)/shard_map/pallas_call | solution.py:321
  1.6 17.1 %all_to_all.5.buffer_ref = bf16[8,136,128]{2,1,0:T(8,128)(2,1)S(1)} all-to-all(bf16[8,136,128]{2,1,0:T(8,128)(2,1)S(1)} %get-tuple-element.18), channel_id=1, replica_groups=mesh['row'=8,'col'=4] {'row'}, dimensions={0} | all-to-all | bytes 557056 | tf_op jit(solution)/shard_map/all_to_all | solution.py:336
  18.7 0.0 copy-start
  18.7 1.6 %collective-permute-start.8 = (bf16[512,128]{1,0:T(8,128)(2,1)S(1)}, bf16[512,128]{1,0:T(8,128)(2,1)S(1)}, u32[]{:S(2)}, u32[]{:S(2)}) collective-permute-start(bf16[512,128]{1,0:T(8,128)(2,1)S(1)} %shard_map.66.local_ref.refs_0_), channel_id=1, source_target_pairs={{0,2},{1,3},{2,0},{3,1},{4,6},{5,7},{6,4},{7,5},{8,10},{9,11},{10,... | collective-permute-start | bytes 393224 | tf_op jit(solution)/shard_map/ppermute | solution.py:281
  20.3 0.0 collective-permute-start.7
  20.3 3.4 %collective-permute-done.8.refs_2_ = bf16[512,128]{1,0:T(8,128)(2,1)S(1)} collective-permute-done((bf16[512,128]{1,0:T(8,128)(2,1)S(1)}, bf16[512,128]{1,0:T(8,128)(2,1)S(1)}, u32[]{:S(2)}, u32[]{:S(2)}) %collective-permute-start.8) | collective-permute-done | bytes 131104 | tf_op jit(solution)/shard_map/ppermute | solution.py:281
  23.8 0.0 collective-permute-start.9
  23.8 0.7 %collective-permute-start = (bf16[96,128]{1,0:T(8,128)(2,1)S(1)}, bf16[96,128]{1,0:T(8,128)(2,1)S(1)}, u32[]{:S(2)}, u32[]{:S(2)}) collective-permute-start(bf16[96,128]{1,0:T(8,128)(2,1)S(1)} %get-tuple-element.13), channel_id=1, source_target_pairs={{0,0},{1,8},{2,16},{3,24},{4,1},{5,9},{6,17},{7,25},{8,2},{9,10},{... | collective-permute-start | bytes 73736 | tf_op jit(solution)/shard_map/ppermute | solution.py:334
  24.4 2.0 %collective-permute-start.1 = (bf16[64,512]{1,0:T(8,128)(2,1)S(1)}, bf16[64,512]{1,0:T(8,128)(2,1)S(1)}, u32[]{:S(2)}, u32[]{:S(2)}) collective-permute-start(bf16[64,512]{1,0:T(8,128)(2,1)S(1)} %get-tuple-element.15), channel_id=1, source_target_pairs={{0,1},{1,0},{2,3},{3,2},{4,5},{5,4},{6,7},{7,6},{8,9},{9,8},{10,11... | collective-permute-start | bytes 196616 | tf_op jit(solution)/shard_map/ppermute | solution.py:281
  26.5 2.3 %collective-permute-start.2 = (bf16[64,512]{1,0:T(8,128)(2,1)S(1)}, bf16[64,512]{1,0:T(8,128)(2,1)S(1)}, u32[]{:S(2)}, u32[]{:S(2)}) collective-permute-start(bf16[64,512]{1,0:T(8,128)(2,1)S(1)} %get-tuple-element.16), channel_id=1, source_target_pairs={{0,2},{1,3},{2,0},{3,1},{4,6},{5,7},{6,4},{7,5},{8,10},{9,11},{10,... | collective-permute-start | bytes 196616 | tf_op jit(solution)/shard_map/ppermute | solution.py:281
  28.8 0.0 collective-permute-done.own_ref
  28.8 0.0 copy-start.1
  28.8 3.7 %collective-permute-start.3 = (bf16[64,512]{1,0:T(8,128)(2,1)S(1)}, bf16[64,512]{1,0:T(8,128)(2,1)S(1)}, u32[]{:S(2)}, u32[]{:S(2)}) collective-permute-start(bf16[64,512]{1,0:T(8,128)(2,1)S(1)} %get-tuple-element.17), channel_id=1, source_target_pairs={{0,3},{1,2},{2,1},{3,0},{4,7},{5,6},{6,5},{7,4},{8,11},{9,10},{10,... | collective-permute-start | bytes 196616 | tf_op jit(solution)/shard_map/ppermute | solution.py:281
  32.4 0.0 copy-done
  32.4 0.8 %shard_map.67.refs_0_ = f32[40,128]{1,0:T(8,128)S(1)} custom-call(bf16[8,136,128]{2,1,0:T(8,128)(2,1)S(1)} %all_to_all.5.buffer_ref, s32[16,128]{1,0:T(8,128)S(1)} %bitcast.3, bf16[512,128]{1,0:T(8,128)(2,1)S(1)} %shard_map.66.local_ref.refs_0_), custom_call_target="tpu_custom_call" | custom-call | flops 1000000 | bytes 1000000 | tf_op jit(solution)/shard_map/pallas_call | solution.py:339
  33.2 0.0 collective-permute-done.1.refs_1_
  33.2 0.0 collective-permute-start.6
  33.3 0.0 collective-permute-done.2.refs_2_
  33.3 1.5 %collective-permute-start.5 = (f32[40,128]{1,0:T(8,128)S(1)}, f32[40,128]{1,0:T(8,128)S(1)}, u32[]{:S(2)}, u32[]{:S(2)}) collective-permute-start(f32[40,128]{1,0:T(8,128)S(1)} %shard_map.67.refs_0_), channel_id=1, source_target_pairs={{0,2},{1,3},{2,0},{3,1},{4,6},{5,7},{6,4},{7,5},{8,10},{9,11},{10,... | collective-permute-start | bytes 61448 | tf_op jit(solution)/shard_map/ppermute | solution.py:281
  34.7 0.3 collective-permute-done.3.refs_3_
  35.1 0.1 collective-permute-start.4
  35.2 0.0 copy-done.1
  35.2 0.3 shard_map.65.edges_ref
  35.5 1.2 %collective-permute-done.6.refs_3_ = f32[40,128]{1,0:T(8,128)S(1)} collective-permute-done((f32[40,128]{1,0:T(8,128)S(1)}, f32[40,128]{1,0:T(8,128)S(1)}, u32[]{:S(2)}, u32[]{:S(2)}) %collective-permute-start.6) | collective-permute-done | bytes 20512 | tf_op jit(solution)/shard_map/ppermute | solution.py:281
  36.7 0.5 %collective-permute-done.5.refs_2_ = f32[40,128]{1,0:T(8,128)S(1)} collective-permute-done((f32[40,128]{1,0:T(8,128)S(1)}, f32[40,128]{1,0:T(8,128)S(1)}, u32[]{:S(2)}, u32[]{:S(2)}) %collective-permute-start.5) | collective-permute-done | bytes 20512 | tf_op jit(solution)/shard_map/ppermute | solution.py:281
  37.1 0.0 collective-permute-done.4.refs_1_
  37.1 0.5 %shard_map.68 = (bf16[64,2048]{1,0:T(8,128)(2,1)S(1)}, f32[64,128]{1,0:T(8,128)S(1)}) custom-call(bf16[96,128]{1,0:T(8,128)(2,1)S(1)} %collective-permute-done.own_ref, s32[16,128]{1,0:T(8,128)S(1)} %bitcast.5, bf16[64,2048]{1,0:T(8,128)(2,1)S(1)} %shard_map.65.edges_ref, f32[40,128]{1,0:T(8,128)S(1)} %shard_map.67.refs_0_, ...), custom_call_target="tpu_custom_call" | custom-call | flops 1000000 | bytes 1000000 | tf_op jit(solution)/shard_map/pallas_call | solution.py:350
  37.6 0.0 collective-permute-done.7.refs_1_
  37.6 0.2 shard_map.69.base_ref
  37.8 0.0 collective-permute-done.9.refs_0_
  37.8 0.8 %shard_map.70 = f32[64,128]{1,0:T(8,128)} custom-call(bf16[64,2048]{1,0:T(8,128)(2,1)S(1)} %get-tuple-element.19.weighted_ref, f32[64,128]{1,0:T(8,128)S(1)} %shard_map.69.base_ref, bf16[512,128]{1,0:T(8,128)(2,1)S(1)} %collective-permute-done.9.refs_0_), custom_call_target="tpu_custom_call" | custom-call | flops 1000000 | bytes 1000000 | tf_op jit(solution)/shard_map/pallas_call | solution.py:360
  (1 shorter events, 0.0 us)
Async XLA Ops:
  18.7 13.7 %copy-start = (s32[2048]{0:T(1024)S(1)}, s32[2048]{0:T(1024)}, u32[]{:S(2)}) copy-start(s32[2048]{0:T(1024)} %param.9) | copy-start | bytes 24580
  18.7 5.0 %collective-permute-start.8 = (bf16[512,128]{1,0:T(8,128)(2,1)S(1)}, bf16[512,128]{1,0:T(8,128)(2,1)S(1)}, u32[]{:S(2)}, u32[]{:S(2)}) collective-permute-start(bf16[512,128]{1,0:T(8,128)(2,1)S(1)} %shard_map.66.local_ref.refs_0_), channel_id=1, source_target_pairs={{0,2},{1,3},{2,0},{3,1},{4,6},{5,7},{6,4},{7,5},{8,10},{9,11},{10,... | collective-permute-start | bytes 393224 | tf_op jit(solution)/shard_map/ppermute | solution.py:281
  20.3 17.3 %collective-permute-start.7 = (bf16[512,128]{1,0:T(8,128)(2,1)S(1)}, bf16[512,128]{1,0:T(8,128)(2,1)S(1)}, u32[]{:S(2)}, u32[]{:S(2)}) collective-permute-start(bf16[512,128]{1,0:T(8,128)(2,1)S(1)} %shard_map.66.local_ref.refs_0_), channel_id=1, source_target_pairs={{0,1},{1,0},{2,3},{3,2},{4,5},{5,4},{6,7},{7,6},{8,9},{9,8},{10,11... | collective-permute-start | bytes 393224 | tf_op jit(solution)/shard_map/ppermute | solution.py:281
  23.8 14.1 %collective-permute-start.9 = (bf16[512,128]{1,0:T(8,128)(2,1)S(1)}, bf16[512,128]{1,0:T(8,128)(2,1)S(1)}, u32[]{:S(2)}, u32[]{:S(2)}) collective-permute-start(bf16[512,128]{1,0:T(8,128)(2,1)S(1)} %collective-permute-done.8.refs_2_), channel_id=1, source_target_pairs={{0,1},{1,0},{2,3},{3,2},{4,5},{5,4},{6,7},{7,6},{8,9},{9,8},{10,11... | collective-permute-start | bytes 393224 | tf_op jit(solution)/shard_map/ppermute | solution.py:281
  23.8 5.0 %collective-permute-start = (bf16[96,128]{1,0:T(8,128)(2,1)S(1)}, bf16[96,128]{1,0:T(8,128)(2,1)S(1)}, u32[]{:S(2)}, u32[]{:S(2)}) collective-permute-start(bf16[96,128]{1,0:T(8,128)(2,1)S(1)} %get-tuple-element.13), channel_id=1, source_target_pairs={{0,0},{1,8},{2,16},{3,24},{4,1},{5,9},{6,17},{7,25},{8,2},{9,10},{... | collective-permute-start | bytes 73736 | tf_op jit(solution)/shard_map/ppermute | solution.py:334
  24.4 8.8 %collective-permute-start.1 = (bf16[64,512]{1,0:T(8,128)(2,1)S(1)}, bf16[64,512]{1,0:T(8,128)(2,1)S(1)}, u32[]{:S(2)}, u32[]{:S(2)}) collective-permute-start(bf16[64,512]{1,0:T(8,128)(2,1)S(1)} %get-tuple-element.15), channel_id=1, source_target_pairs={{0,1},{1,0},{2,3},{3,2},{4,5},{5,4},{6,7},{7,6},{8,9},{9,8},{10,11... | collective-permute-start | bytes 196616 | tf_op jit(solution)/shard_map/ppermute | solution.py:281
  26.5 6.8 %collective-permute-start.2 = (bf16[64,512]{1,0:T(8,128)(2,1)S(1)}, bf16[64,512]{1,0:T(8,128)(2,1)S(1)}, u32[]{:S(2)}, u32[]{:S(2)}) collective-permute-start(bf16[64,512]{1,0:T(8,128)(2,1)S(1)} %get-tuple-element.16), channel_id=1, source_target_pairs={{0,2},{1,3},{2,0},{3,1},{4,6},{5,7},{6,4},{7,5},{8,10},{9,11},{10,... | collective-permute-start | bytes 196616 | tf_op jit(solution)/shard_map/ppermute | solution.py:281
  28.8 6.4 %copy-start.1 = (s32[2048]{0:T(1024)S(1)}, s32[2048]{0:T(1024)}, u32[]{:S(2)}) copy-start(s32[2048]{0:T(1024)} %param.10) | copy-start | bytes 24580
  28.8 6.3 %collective-permute-start.3 = (bf16[64,512]{1,0:T(8,128)(2,1)S(1)}, bf16[64,512]{1,0:T(8,128)(2,1)S(1)}, u32[]{:S(2)}, u32[]{:S(2)}) collective-permute-start(bf16[64,512]{1,0:T(8,128)(2,1)S(1)} %get-tuple-element.17), channel_id=1, source_target_pairs={{0,3},{1,2},{2,1},{3,0},{4,7},{5,6},{6,5},{7,4},{8,11},{9,10},{10,... | collective-permute-start | bytes 196616 | tf_op jit(solution)/shard_map/ppermute | solution.py:281
  33.2 3.4 %collective-permute-start.6 = (f32[40,128]{1,0:T(8,128)S(1)}, f32[40,128]{1,0:T(8,128)S(1)}, u32[]{:S(2)}, u32[]{:S(2)}) collective-permute-start(f32[40,128]{1,0:T(8,128)S(1)} %shard_map.67.refs_0_), channel_id=1, source_target_pairs={{0,3},{1,2},{2,1},{3,0},{4,7},{5,6},{6,5},{7,4},{8,11},{9,10},{10,... | collective-permute-start | bytes 61448 | tf_op jit(solution)/shard_map/ppermute | solution.py:281
  33.3 3.9 %collective-permute-start.5 = (f32[40,128]{1,0:T(8,128)S(1)}, f32[40,128]{1,0:T(8,128)S(1)}, u32[]{:S(2)}, u32[]{:S(2)}) collective-permute-start(f32[40,128]{1,0:T(8,128)S(1)} %shard_map.67.refs_0_), channel_id=1, source_target_pairs={{0,2},{1,3},{2,0},{3,1},{4,6},{5,7},{6,4},{7,5},{8,10},{9,11},{10,... | collective-permute-start | bytes 61448 | tf_op jit(solution)/shard_map/ppermute | solution.py:281
  35.1 2.1 %collective-permute-start.4 = (f32[40,128]{1,0:T(8,128)S(1)}, f32[40,128]{1,0:T(8,128)S(1)}, u32[]{:S(2)}, u32[]{:S(2)}) collective-permute-start(f32[40,128]{1,0:T(8,128)S(1)} %shard_map.67.refs_0_), channel_id=1, source_target_pairs={{0,1},{1,0},{2,3},{3,2},{4,5},{5,4},{6,7},{7,6},{8,9},{9,8},{10,11... | collective-permute-start | bytes 61448 | tf_op jit(solution)/shard_map/ppermute | solution.py:281

commit v4 on v3

--- a/solution.py
+++ b/solution.py
@@ -66,6 +66,12 @@
         self.at_extra = self.at_counts + self.units * self.row_hosts
         self.payload = self.at_extra + 8
         self.extra = (self.units + 1 + 7) // 8 * 8
+
+    def row_at(self, place):
+        return (place + self.rows // 2) % self.rows
+
+    def place_of(self, row):
+        return (row - self.rows // 2) % self.rows
 
 
 def rows_of(row, half, piece):
@@ -165,21 +171,21 @@
 
 def ranks_kernel(s, buffer_ref, local_ref):
     for n in range(s.rows):
-        local_ref[n * s.piece : (n + 1) * s.piece, :] = buffer_ref[n, : s.piece, :]
+        local_ref[n * s.piece : (n + 1) * s.piece, :] = buffer_ref[s.place_of(n), : s.piece, :]
 
 
 def graph_kernel(s, buffer_ref, hosts_ref, local_ref, shared_ref):
     column = lax.axis_index("col")
     ones = jnp.ones((8, LANES), bf16)
     low = iota((1, LANES), 1) < s.piece
-    extras = [buffer_ref[n, s.at_extra :, :].astype(f32) for n in range(s.rows)]
+    extras = [buffer_ref[s.place_of(n), s.at_extra :, :].astype(f32) for n in range(s.rows)]
     total = functools.reduce(jnp.add, [e[1:2] + e[2:3] for e in extras])
     for m in range(s.units):
         unit = column * s.units + m
         member = members(hosts_ref[pl.ds(unit, 1), :], unit * s.unit_hosts, s.unit_hosts)
         start = s.at_counts + m * s.row_hosts
         counts = jnp.concatenate(
-            [buffer_ref[n, start : start + s.row_hosts, :] for n in range(s.rows)], axis=0
+            [buffer_ref[s.place_of(n), start : start + s.row_hosts, :] for n in range(s.rows)], axis=0
         )
         ranks = local_ref[m * s.tile : (m + 1) * s.tile, :]
         inward = jnp.where(low, extras[s.pair * m][:1], extras[s.pair * m + 1][:1])
@@ -196,26 +202,32 @@
     shared_ref[s.column_hosts + s.units : s.column_hosts + s.units + 1, : s.topics] = total
 
 
-def edges_kernel(s, own_ref, hosts_ref, dangling_ref, *refs):
-    chunk_refs, out_ref = refs[: s.cols], refs[s.cols]
-    row, column = lax.axis_index("row"), lax.axis_index("col")
-    for k in range(s.cols):
-        at = pl.multiple_of((column ^ k) * s.width, s.width)
-        out_ref[:, pl.ds(at, s.width)] = chunk_refs[k][...]
-    piece = row * s.cols + column
+def mask_kernel(s, hosts_ref, dangling_ref, out_ref):
+    piece = lax.axis_index("row") * s.cols + lax.axis_index("col")
     unit, half = piece // s.pair, piece % s.pair
     hosts = hosts_ref[pl.ds(unit, 1), :]
     keep = dangling_ref[pl.ds(unit, 1), :] == 0
     mine = rows_of(hosts, half, s.piece)[:, : s.piece]
     first = piece * HOSTS_PIECE
-    same = mm_tn(members(mine, first, 8).astype(bf16), members(hosts, first, 8).astype(bf16)) > 0
+    same = mm_tn(members(mine, first, 8).astype(bf16), members(hosts, first, 8).astype(bf16))
+    out_ref[...] = same * jnp.where(keep, 1.0, -1.0)
+
+
+def edges_kernel(s, own_ref, mask_ref, *refs):
+    chunk_refs, out_ref = refs[: s.cols], refs[s.cols]
+    column = lax.axis_index("col")
+    for k in range(s.cols):
+        at = pl.multiple_of((column ^ k) * s.width, s.width)
+        out_ref[:, pl.ds(at, s.width)] = chunk_refs[k][...]
+    unit = (lax.axis_index("row") * s.cols + column) // s.pair
+    mask = mask_ref[...]
     packed = own_ref[s.piece :, :].astype(f32)
     rolled = pltpu.roll(packed, s.piece, 1)
     low = iota((s.packed, LANES), 1) < s.piece
     local = jnp.concatenate([jnp.where(low, packed, rolled), jnp.where(low, rolled, packed)], axis=0)
     at = pl.multiple_of(unit * s.tile, s.tile)
     across = out_ref[:, pl.ds(at, s.tile)].astype(f32)
-    fixed = jnp.where(same, jnp.where(keep, local, 0.0), across)
+    fixed = jnp.where(mask == 0, across, jnp.where(mask > 0, local, 0.0))
     out_ref[:, pl.ds(at, s.tile)] = fixed.astype(bf16)
 
 
@@ -333,7 +345,8 @@
     moves = [(r * cols + c, c * rows + r) for r in range(rows) for c in range(cols)]
     own = lax.ppermute(own, ("row", "col"), moves)
     chunks = spread(chunks, cols)
-    held = lax.all_to_all(sent, "row", 0, 0, tiled=True)
+    group = [s.row_at(p) for p in range(rows)]
+    held = lax.all_to_all(sent, "row", 0, 0, tiled=True, axis_index_groups=[group])
     local = call(functools.partial(ranks_kernel, s), shape((s.width, s.topics), bf16), [VMEM])(held)
     locals_ = gathered(local, cols)
     shared = call(
@@ -342,11 +355,14 @@
         [VMEM] * 3,
     )(held, hosts, local)
     shared = spread([shared] * cols, cols)
+    mask = call(
+        functools.partial(mask_kernel, s), shape((s.piece, s.tile), f32), [VMEM] * 2
+    )(hosts, ignored)
     edges = call(
         functools.partial(edges_kernel, s),
         shape((s.piece, pages), bf16),
-        [VMEM] * (3 + cols),
-    )(own, hosts, ignored, *chunks)
+        [VMEM] * (2 + cols),
+    )(own, mask, *chunks)
     weighted, base = call(
         functools.partial(host_kernel, s),
         (shape((s.piece, pages), bf16), shape((s.piece, s.topics), f32)),

time: 38.9 us -> 38.2 us (0.982)
  blocking collectives: 17.1 us -> 15.3 us
  waiting for transfers between devices: 5.46 us -> 6.25 us
    all_to_all x1, blocking collectives: 17.1 us -> 15.3 us  [on_device(): lax.all_to_all(sent, 'row', 0, 0, tiled=True, axis_index_groups=[group])]
    ppermute x9, waiting for transfers between devices: 5.46 us -> 6.25 us  [swap(): return lax.ppermute(x, 'col', [(i, i ^ bits) for i in range(count)])]
  transfers between devices with their start and end apart: 10 -> 10, of which waited for: 4 -> 4; matrix products, arithmetic and copies ran while one was open for 0% -> 0% of each run, Pallas kernels for 4% -> 5%
where the time goes in v4:
time: 38.2 us; the launch traced here: 38 us
  blocking collectives  15.3 us (40%)
  starting transfers between devices  12.1 us (32%)
  waiting for transfers between devices  6.25 us (16%)
  Pallas kernels  4.16 us (11%)
    all_to_all x1, blocking collectives, on_device(): lax.all_to_all(sent, 'row', 0, 0, tiled=True, axis_index_groups=[group])  15.3 us
    ppermute x9, starting transfers between devices, swap(): return lax.ppermute(x, 'col', [(i, i ^ bits) for i in range(count)])  11.5 us
    ppermute x9, waiting for transfers between devices, swap(): return lax.ppermute(x, 'col', [(i, i ^ bits) for i in range(count)])  6.25 us
    pallas_call x1, Pallas kernels, on_device(): call(functools.partial(first_kernel, s), (shape((rows, s.payload, LANES),...  1.58 us
    pallas_call x2, Pallas kernels, on_device(): call(functools.partial(flow_kernel, s, distances), shape((s.piece, s.topi...  0.98 us
    pallas_call x1, Pallas kernels, on_device(): call(functools.partial(graph_kernel, s), shape((s.column_hosts + s.extra,...  0.77 us
  transfers between devices with their start and end apart: 10, of which 4 were waited for; matrix products, arithmetic and copies ran while one was open for 0% of the time, Pallas kernels for 5%

profile of v4, /device:TPU:0, one launch (start us, length us, event | category | flops | bytes accessed | tf_op | source)
XLA Modules:
  0.0 38.0 jit_solution(2329458468703928911)
XLA Ops:
  0.0 1.6 %shard_map.64 = (bf16[8,136,128]{2,1,0:T(8,128)(2,1)S(1)}, bf16[96,128]{1,0:T(8,128)(2,1)S(1)}, bf16[64,512]{1,0:T(8,128)(2,1)S(1)}, bf16[64,512]{1,0:T(8,128)(2...) custom-call(s32[2,4]{1,0:T(2,128)} %tiles_hbm.1, bf16[256,512]{1,0:T(8,128)(2,1)} %links_hbm.1, ...), custom_call_target="tpu_custom_call" | custom-call | flops 1000000 | bytes 1000000 | tf_op jit(solution)/shard_map/pallas_call | solution.py:333
  1.6 15.3 %all_to_all.5.buffer_ref = bf16[8,136,128]{2,1,0:T(8,128)(2,1)S(1)} all-to-all(bf16[8,136,128]{2,1,0:T(8,128)(2,1)S(1)} %get-tuple-element.18), channel_id=1, replica_groups={{16,20,24,28,0,4,8,12},{17,21,25,29,1,5,9,13},{18,22,26,30,2,6,10,14},{..., dimensions={0} | all-to-all | bytes 557056 | tf_op jit(solution)/shard_map/all_to_all | solution.py:349
  16.9 0.0 copy-start
  16.9 1.6 %collective-permute-start.8 = (bf16[512,128]{1,0:T(8,128)(2,1)S(1)}, bf16[512,128]{1,0:T(8,128)(2,1)S(1)}, u32[]{:S(2)}, u32[]{:S(2)}) collective-permute-start(bf16[512,128]{1,0:T(8,128)(2,1)S(1)} %shard_map.67.local_ref.refs_0_), channel_id=1, source_target_pairs={{0,2},{1,3},{2,0},{3,1},{4,6},{5,7},{6,4},{7,5},{8,10},{9,11},{10,... | collective-permute-start | bytes 393224 | tf_op jit(solution)/shard_map/ppermute | solution.py:293
  18.5 0.0 collective-permute-start.7
  18.5 3.4 %collective-permute-done.8.refs_2_ = bf16[512,128]{1,0:T(8,128)(2,1)S(1)} collective-permute-done((bf16[512,128]{1,0:T(8,128)(2,1)S(1)}, bf16[512,128]{1,0:T(8,128)(2,1)S(1)}, u32[]{:S(2)}, u32[]{:S(2)}) %collective-permute-start.8) | collective-permute-done | bytes 131104 | tf_op jit(solution)/shard_map/ppermute | solution.py:293
  22.0 0.0 collective-permute-start.9
  22.0 0.7 %collective-permute-start = (bf16[96,128]{1,0:T(8,128)(2,1)S(1)}, bf16[96,128]{1,0:T(8,128)(2,1)S(1)}, u32[]{:S(2)}, u32[]{:S(2)}) collective-permute-start(bf16[96,128]{1,0:T(8,128)(2,1)S(1)} %get-tuple-element.13), channel_id=1, source_target_pairs={{0,0},{1,8},{2,16},{3,24},{4,1},{5,9},{6,17},{7,25},{8,2},{9,10},{... | collective-permute-start | bytes 73736 | tf_op jit(solution)/shard_map/ppermute | solution.py:346
  22.6 2.0 %collective-permute-start.1 = (bf16[64,512]{1,0:T(8,128)(2,1)S(1)}, bf16[64,512]{1,0:T(8,128)(2,1)S(1)}, u32[]{:S(2)}, u32[]{:S(2)}) collective-permute-start(bf16[64,512]{1,0:T(8,128)(2,1)S(1)} %get-tuple-element.15), channel_id=1, source_target_pairs={{0,1},{1,0},{2,3},{3,2},{4,5},{5,4},{6,7},{7,6},{8,9},{9,8},{10,11... | collective-permute-start | bytes 196616 | tf_op jit(solution)/shard_map/ppermute | solution.py:293
  24.7 3.2 %collective-permute-start.2 = (bf16[64,512]{1,0:T(8,128)(2,1)S(1)}, bf16[64,512]{1,0:T(8,128)(2,1)S(1)}, u32[]{:S(2)}, u32[]{:S(2)}) collective-permute-start(bf16[64,512]{1,0:T(8,128)(2,1)S(1)} %get-tuple-element.16), channel_id=1, source_target_pairs={{0,2},{1,3},{2,0},{3,1},{4,6},{5,7},{6,4},{7,5},{8,10},{9,11},{10,... | collective-permute-start | bytes 196616 | tf_op jit(solution)/shard_map/ppermute | solution.py:293
  27.9 0.0 collective-permute-done.own_ref
  27.9 0.0 copy-start.1
  27.9 2.7 %collective-permute-start.3 = (bf16[64,512]{1,0:T(8,128)(2,1)S(1)}, bf16[64,512]{1,0:T(8,128)(2,1)S(1)}, u32[]{:S(2)}, u32[]{:S(2)}) collective-permute-start(bf16[64,512]{1,0:T(8,128)(2,1)S(1)} %get-tuple-element.17), channel_id=1, source_target_pairs={{0,3},{1,2},{2,1},{3,0},{4,7},{5,6},{6,5},{7,4},{8,11},{9,10},{10,... | collective-permute-start | bytes 196616 | tf_op jit(solution)/shard_map/ppermute | solution.py:293
  30.6 0.0 copy-done
  30.6 0.8 %shard_map.68.refs_0_ = f32[40,128]{1,0:T(8,128)S(1)} custom-call(bf16[8,136,128]{2,1,0:T(8,128)(2,1)S(1)} %all_to_all.5.buffer_ref, s32[16,128]{1,0:T(8,128)S(1)} %bitcast.3, bf16[512,128]{1,0:T(8,128)(2,1)S(1)} %shard_map.67.local_ref.refs_0_), custom_call_target="tpu_custom_call" | custom-call | flops 1000000 | bytes 1000000 | tf_op jit(solution)/shard_map/pallas_call | solution.py:352
  31.4 0.0 collective-permute-done.1.refs_1_
  31.4 0.0 collective-permute-start.4
  31.5 0.0 collective-permute-done.2.refs_2_
  31.5 0.8 %collective-permute-start.5 = (f32[40,128]{1,0:T(8,128)S(1)}, f32[40,128]{1,0:T(8,128)S(1)}, u32[]{:S(2)}, u32[]{:S(2)}) collective-permute-start(f32[40,128]{1,0:T(8,128)S(1)} %shard_map.68.refs_0_), channel_id=1, source_target_pairs={{0,2},{1,3},{2,0},{3,1},{4,6},{5,7},{6,4},{7,5},{8,10},{9,11},{10,... | collective-permute-start | bytes 61448 | tf_op jit(solution)/shard_map/ppermute | solution.py:293
  32.2 1.0 %collective-permute-done.3.refs_3_ = bf16[64,512]{1,0:T(8,128)(2,1)S(1)} collective-permute-done((bf16[64,512]{1,0:T(8,128)(2,1)S(1)}, bf16[64,512]{1,0:T(8,128)(2,1)S(1)}, u32[]{:S(2)}, u32[]{:S(2)}) %collective-permute-start.3) | collective-permute-done | bytes 65568 | tf_op jit(solution)/shard_map/ppermute | solution.py:293
  33.3 1.1 %collective-permute-start.6 = (f32[40,128]{1,0:T(8,128)S(1)}, f32[40,128]{1,0:T(8,128)S(1)}, u32[]{:S(2)}, u32[]{:S(2)}) collective-permute-start(f32[40,128]{1,0:T(8,128)S(1)} %shard_map.68.refs_0_), channel_id=1, source_target_pairs={{0,3},{1,2},{2,1},{3,0},{4,7},{5,6},{6,5},{7,4},{8,11},{9,10},{10,... | collective-permute-start | bytes 61448 | tf_op jit(solution)/shard_map/ppermute | solution.py:293
  34.4 0.0 copy-done.1
  34.4 0.3 shard_map.65.mask_ref
  34.6 0.1 shard_map.66.edges_ref
  34.7 0.0 collective-permute-done.4.refs_1_
  34.7 0.6 %collective-permute-done.5.refs_2_ = f32[40,128]{1,0:T(8,128)S(1)} collective-permute-done((f32[40,128]{1,0:T(8,128)S(1)}, f32[40,128]{1,0:T(8,128)S(1)}, u32[]{:S(2)}, u32[]{:S(2)}) %collective-permute-start.5) | collective-permute-done | bytes 20512 | tf_op jit(solution)/shard_map/ppermute | solution.py:293
  35.3 1.2 %collective-permute-done.6.refs_3_ = f32[40,128]{1,0:T(8,128)S(1)} collective-permute-done((f32[40,128]{1,0:T(8,128)S(1)}, f32[40,128]{1,0:T(8,128)S(1)}, u32[]{:S(2)}, u32[]{:S(2)}) %collective-permute-start.6) | collective-permute-done | bytes 20512 | tf_op jit(solution)/shard_map/ppermute | solution.py:293
  36.5 0.5 %shard_map.69 = (bf16[64,2048]{1,0:T(8,128)(2,1)S(1)}, f32[64,128]{1,0:T(8,128)S(1)}) custom-call(bf16[96,128]{1,0:T(8,128)(2,1)S(1)} %collective-permute-done.own_ref, s32[16,128]{1,0:T(8,128)S(1)} %bitcast.5, bf16[64,2048]{1,0:T(8,128)(2,1)S(1)} %shard_map.66.edges_ref, f32[40,128]{1,0:T(8,128)S(1)} %shard_map.68.refs_0_, ...), custom_call_target="tpu_custom_call" | custom-call | flops 1000000 | bytes 1000000 | tf_op jit(solution)/shard_map/pallas_call | solution.py:366
  37.0 0.0 collective-permute-done.7.refs_1_
  37.0 0.2 shard_map.70.base_ref
  37.2 0.0 collective-permute-done.9.refs_0_
  37.2 0.8 %shard_map.71 = f32[64,128]{1,0:T(8,128)} custom-call(bf16[64,2048]{1,0:T(8,128)(2,1)S(1)} %get-tuple-element.19.weighted_ref, f32[64,128]{1,0:T(8,128)S(1)} %shard_map.70.base_ref, bf16[512,128]{1,0:T(8,128)(2,1)S(1)} %collective-permute-done.9.refs_0_), custom_call_target="tpu_custom_call" | custom-call | flops 1000000 | bytes 1000000 | tf_op jit(solution)/shard_map/pallas_call | solution.py:376
  (1 shorter events, 0.0 us)
Async XLA Ops:
  16.9 13.7 %copy-start = (s32[2048]{0:T(1024)S(1)}, s32[2048]{0:T(1024)}, u32[]{:S(2)}) copy-start(s32[2048]{0:T(1024)} %param.9) | copy-start | bytes 24580
  16.9 5.0 %collective-permute-start.8 = (bf16[512,128]{1,0:T(8,128)(2,1)S(1)}, bf16[512,128]{1,0:T(8,128)(2,1)S(1)}, u32[]{:S(2)}, u32[]{:S(2)}) collective-permute-start(bf16[512,128]{1,0:T(8,128)(2,1)S(1)} %shard_map.67.local_ref.refs_0_), channel_id=1, source_target_pairs={{0,2},{1,3},{2,0},{3,1},{4,6},{5,7},{6,4},{7,5},{8,10},{9,11},{10,... | collective-permute-start | bytes 393224 | tf_op jit(solution)/shard_map/ppermute | solution.py:293
  18.5 18.4 %collective-permute-start.7 = (bf16[512,128]{1,0:T(8,128)(2,1)S(1)}, bf16[512,128]{1,0:T(8,128)(2,1)S(1)}, u32[]{:S(2)}, u32[]{:S(2)}) collective-permute-start(bf16[512,128]{1,0:T(8,128)(2,1)S(1)} %shard_map.67.local_ref.refs_0_), channel_id=1, source_target_pairs={{0,1},{1,0},{2,3},{3,2},{4,5},{5,4},{6,7},{7,6},{8,9},{9,8},{10,11... | collective-permute-start | bytes 393224 | tf_op jit(solution)/shard_map/ppermute | solution.py:293
  22.0 15.2 %collective-permute-start.9 = (bf16[512,128]{1,0:T(8,128)(2,1)S(1)}, bf16[512,128]{1,0:T(8,128)(2,1)S(1)}, u32[]{:S(2)}, u32[]{:S(2)}) collective-permute-start(bf16[512,128]{1,0:T(8,128)(2,1)S(1)} %collective-permute-done.8.refs_2_), channel_id=1, source_target_pairs={{0,1},{1,0},{2,3},{3,2},{4,5},{5,4},{6,7},{7,6},{8,9},{9,8},{10,11... | collective-permute-start | bytes 393224 | tf_op jit(solution)/shard_map/ppermute | solution.py:293
  22.0 5.9 %collective-permute-start = (bf16[96,128]{1,0:T(8,128)(2,1)S(1)}, bf16[96,128]{1,0:T(8,128)(2,1)S(1)}, u32[]{:S(2)}, u32[]{:S(2)}) collective-permute-start(bf16[96,128]{1,0:T(8,128)(2,1)S(1)} %get-tuple-element.13), channel_id=1, source_target_pairs={{0,0},{1,8},{2,16},{3,24},{4,1},{5,9},{6,17},{7,25},{8,2},{9,10},{... | collective-permute-start | bytes 73736 | tf_op jit(solution)/shard_map/ppermute | solution.py:346
  22.6 8.8 %collective-permute-start.1 = (bf16[64,512]{1,0:T(8,128)(2,1)S(1)}, bf16[64,512]{1,0:T(8,128)(2,1)S(1)}, u32[]{:S(2)}, u32[]{:S(2)}) collective-permute-start(bf16[64,512]{1,0:T(8,128)(2,1)S(1)} %get-tuple-element.15), channel_id=1, source_target_pairs={{0,1},{1,0},{2,3},{3,2},{4,5},{5,4},{6,7},{7,6},{8,9},{9,8},{10,11... | collective-permute-start | bytes 196616 | tf_op jit(solution)/shard_map/ppermute | solution.py:293
  24.7 6.8 %collective-permute-start.2 = (bf16[64,512]{1,0:T(8,128)(2,1)S(1)}, bf16[64,512]{1,0:T(8,128)(2,1)S(1)}, u32[]{:S(2)}, u32[]{:S(2)}) collective-permute-start(bf16[64,512]{1,0:T(8,128)(2,1)S(1)} %get-tuple-element.16), channel_id=1, source_target_pairs={{0,2},{1,3},{2,0},{3,1},{4,6},{5,7},{6,4},{7,5},{8,10},{9,11},{10,... | collective-permute-start | bytes 196616 | tf_op jit(solution)/shard_map/ppermute | solution.py:293
  27.9 6.5 %copy-start.1 = (s32[2048]{0:T(1024)S(1)}, s32[2048]{0:T(1024)}, u32[]{:S(2)}) copy-start(s32[2048]{0:T(1024)} %param.10) | copy-start | bytes 24580
  27.9 5.4 %collective-permute-start.3 = (bf16[64,512]{1,0:T(8,128)(2,1)S(1)}, bf16[64,512]{1,0:T(8,128)(2,1)S(1)}, u32[]{:S(2)}, u32[]{:S(2)}) collective-permute-start(bf16[64,512]{1,0:T(8,128)(2,1)S(1)} %get-tuple-element.17), channel_id=1, source_target_pairs={{0,3},{1,2},{2,1},{3,0},{4,7},{5,6},{6,5},{7,4},{8,11},{9,10},{10,... | collective-permute-start | bytes 196616 | tf_op jit(solution)/shard_map/ppermute | solution.py:293
  31.4 3.3 %collective-permute-start.4 = (f32[40,128]{1,0:T(8,128)S(1)}, f32[40,128]{1,0:T(8,128)S(1)}, u32[]{:S(2)}, u32[]{:S(2)}) collective-permute-start(f32[40,128]{1,0:T(8,128)S(1)} %shard_map.68.refs_0_), channel_id=1, source_target_pairs={{0,1},{1,0},{2,3},{3,2},{4,5},{5,4},{6,7},{7,6},{8,9},{9,8},{10,11... | collective-permute-start | bytes 61448 | tf_op jit(solution)/shard_map/ppermute | solution.py:293
  31.5 3.8 %collective-permute-start.5 = (f32[40,128]{1,0:T(8,128)S(1)}, f32[40,128]{1,0:T(8,128)S(1)}, u32[]{:S(2)}, u32[]{:S(2)}) collective-permute-start(f32[40,128]{1,0:T(8,128)S(1)} %shard_map.68.refs_0_), channel_id=1, source_target_pairs={{0,2},{1,3},{2,0},{3,1},{4,6},{5,7},{6,4},{7,5},{8,10},{9,11},{10,... | collective-permute-start | bytes 61448 | tf_op jit(solution)/shard_map/ppermute | solution.py:293
  33.3 3.2 %collective-permute-start.6 = (f32[40,128]{1,0:T(8,128)S(1)}, f32[40,128]{1,0:T(8,128)S(1)}, u32[]{:S(2)}, u32[]{:S(2)}) collective-permute-start(f32[40,128]{1,0:T(8,128)S(1)} %shard_map.68.refs_0_), channel_id=1, source_target_pairs={{0,3},{1,2},{2,1},{3,0},{4,7},{5,6},{6,5},{7,4},{8,11},{9,10},{10,... | collective-permute-start | bytes 61448 | tf_op jit(solution)/shard_map/ppermute | solution.py:293

commit v5 on v4

--- a/solution.py
+++ b/solution.py
@@ -65,7 +65,7 @@
         self.at_counts = self.piece
         self.at_extra = self.at_counts + self.units * self.row_hosts
         self.payload = self.at_extra + 8
-        self.extra = (self.units + 1 + 7) // 8 * 8
+        self.extra = (2 * self.units + 2 + 15) // 16 * 16
 
     def row_at(self, place):
         return (place + self.rows // 2) % self.rows
@@ -176,10 +176,12 @@
 
 def graph_kernel(s, buffer_ref, hosts_ref, local_ref, shared_ref):
     column = lax.axis_index("col")
-    ones = jnp.ones((8, LANES), bf16)
     low = iota((1, LANES), 1) < s.piece
     extras = [buffer_ref[s.place_of(n), s.at_extra :, :].astype(f32) for n in range(s.rows)]
     total = functools.reduce(jnp.add, [e[1:2] + e[2:3] for e in extras])
+    square = (s.tile, s.tile)
+    diagonal = iota(square, 0) == iota(square, 1)
+    lines = []
     for m in range(s.units):
         unit = column * s.units + m
         member = members(hosts_ref[pl.ds(unit, 1), :], unit * s.unit_hosts, s.unit_hosts)
@@ -187,19 +189,27 @@
         counts = jnp.concatenate(
             [buffer_ref[s.place_of(n), start : start + s.row_hosts, :] for n in range(s.rows)], axis=0
         )
-        ranks = local_ref[m * s.tile : (m + 1) * s.tile, :]
-        inward = jnp.where(low, extras[s.pair * m][:1], extras[s.pair * m + 1][:1])
-        degree = inward + mm(jnp.ones((8, s.hosts), bf16), counts)[:1]
+        extra = jnp.where(low, extras[s.pair * m], extras[s.pair * m + 1])
+        outward = jnp.sum(counts.astype(f32), axis=0, keepdims=True)
+        degree = extra[:1] + outward
         has_out = degree > 0
         inverse = jnp.where(has_out, 1.0 / jnp.where(has_out, degree, 1.0), 0.0)
-        means = mm_nt(ones[:, : s.topics], ranks)[:1] * (1.0 / s.topics) * inverse
-        weights = mm_nt((member.astype(f32) * means).astype(bf16), counts)
-        out = jnp.sum(weights, axis=1, keepdims=True)
+        ranks = local_ref[m * s.tile : (m + 1) * s.tile, :].astype(f32)
+        sums = jnp.sum(ranks, axis=1, keepdims=True)
+        sums = jnp.sum(jnp.where(diagonal, sums, 0.0), axis=0, keepdims=True)
+        means = sums * (1.0 / s.topics) * inverse
+        spread = (member.astype(f32) * means).astype(bf16)
+        weights = mm_nt(spread, counts)
+        out = jnp.sum(spread.astype(f32) * outward, axis=1, keepdims=True)
         linked = out > 0
-        norm = jnp.where(linked, weights / jnp.where(linked, out, 1.0), 1.0 / s.hosts)
-        shared_ref[m * s.unit_hosts : (m + 1) * s.unit_hosts, :] = norm
-        shared_ref[s.column_hosts + m : s.column_hosts + m + 1, :LANES] = inverse
-    shared_ref[s.column_hosts + s.units : s.column_hosts + s.units + 1, : s.topics] = total
+        norm = jnp.where(linked, weights * (1.0 / jnp.where(linked, out, 1.0)), 1.0 / s.hosts)
+        shared_ref[m * s.unit_hosts : (m + 1) * s.unit_hosts, :] = norm.astype(bf16)
+        high = inverse.astype(bf16).astype(f32)
+        lines += [high, inverse - high]
+    high = total.astype(bf16).astype(f32)
+    lines += [high, total - high]
+    lines += [jnp.zeros((1, LANES), f32)] * (s.extra - len(lines))
+    shared_ref[s.column_hosts :, :LANES] = jnp.concatenate(lines, axis=0).astype(bf16)
 
 
 def mask_kernel(s, hosts_ref, dangling_ref, out_ref):
@@ -247,17 +257,18 @@
     for k in range(s.cols):
         at = pl.multiple_of((column ^ k) * s.column_hosts, s.column_hosts)
         full_ref[pl.ds(at, s.column_hosts), :] = shared[k][: s.column_hosts, :]
-        end = s.column_hosts + s.units
-        inverse_ref[pl.ds((column ^ k) * s.units, s.units), :] = shared[k][s.column_hosts : end, :LANES]
-        total = total + shared[k][end : end + 1, : s.topics]
+        lines = shared[k][s.column_hosts :, :LANES].astype(f32)
+        for m in range(s.units):
+            line = lines[2 * m : 2 * m + 1] + lines[2 * m + 1 : 2 * m + 2]
+            inverse_ref[pl.ds((column ^ k) * s.units + m, 1), :] = line
+        total = total + lines[2 * s.units : 2 * s.units + 1] + lines[2 * s.units + 1 : 2 * s.units + 2]
     base_ref[...] = (1 - damping) * s.pages * own_ref[: s.piece, :].astype(f32) / total
     norm = full_ref[...]
-    norm_high, norm_low = split(norm)
-    rank = damping * jnp.sum(norm, axis=0, keepdims=True) + (1 - damping)
-    for _ in range(HOST_ITERS - 1):
-        parts = three(rank)
-        fresh = mm(parts, norm_high) + mm(parts, norm_low)
-        rank = damping * jnp.sum(fresh, axis=0, keepdims=True) + (1 - damping)
+    parts = jnp.where(iota((8, s.hosts), 0) == 0, 1.0, 0.0).astype(bf16)
+    for step in range(HOST_ITERS):
+        if step:
+            parts = three(rank)
+        rank = damping * jnp.sum(mm(parts, norm), axis=0, keepdims=True) + (1 - damping)
     block = LANES // s.unit_hosts
     all_units = s.units * s.cols
     for g in range(s.hosts // LANES):
@@ -351,7 +362,7 @@
     locals_ = gathered(local, cols)
     shared = call(
         functools.partial(graph_kernel, s),
-        shape((s.column_hosts + s.extra, s.hosts), f32),
+        shape((s.column_hosts + s.extra, s.hosts), bf16),
         [VMEM] * 3,
     )(held, hosts, local)
     shared = spread([shared] * cols, cols)
@@ -367,7 +378,7 @@
         functools.partial(host_kernel, s),
         (shape((s.piece, pages), bf16), shape((s.piece, s.topics), f32)),
         [VMEM] * (3 + cols),
-        [pltpu.VMEM((s.hosts, s.hosts), f32), pltpu.VMEM((s.units * cols, LANES), f32)],
+        [pltpu.VMEM((s.hosts, s.hosts), bf16), pltpu.VMEM((s.units * cols, LANES), f32)],
     )(own, hosts, edges, *shared)
     late = [k for k in range(cols) if k % 2 and k > 1]
     soon = [k for k in range(cols) if k not in late]

time: 38.2 us -> 38.2 us (level)
  starting transfers between devices: 12.1 us -> 12.7 us
  Pallas kernels: 4.16 us -> 3.72 us
    ppermute x9, starting transfers between devices: 11.5 us -> 12.1 us  [swap(): return lax.ppermute(x, 'col', [(i, i ^ bits) for i in range(count)])]
    pallas_call x1, Pallas kernels: 0.77 us -> 0.26 us  [on_device(): call(functools.partial(graph_kernel, s), shape((s.column_hosts + s.extra,...]
  transfers between devices with their start and end apart: 10 -> 10, of which waited for: 4 -> 3; matrix products, arithmetic and copies ran while one was open for 0% -> 0% of each run, Pallas kernels for 5% -> 4%
where the time goes in v5:
time: 38.2 us; the launch traced here: 38 us
  blocking collectives  15.3 us (40%)
  starting transfers between devices  12.7 us (33%)
  waiting for transfers between devices  6.08 us (16%)
  Pallas kernels  3.72 us (10%)
    all_to_all x1, blocking collectives, on_device(): lax.all_to_all(sent, 'row', 0, 0, tiled=True, axis_index_groups=[group])  15.3 us
    ppermute x9, starting transfers between devices, swap(): return lax.ppermute(x, 'col', [(i, i ^ bits) for i in range(count)])  12.1 us
    ppermute x9, waiting for transfers between devices, swap(): return lax.ppermute(x, 'col', [(i, i ^ bits) for i in range(count)])  6.08 us
    pallas_call x1, Pallas kernels, on_device(): call(functools.partial(first_kernel, s), (shape((rows, s.payload, LANES),...  1.58 us
    pallas_call x2, Pallas kernels, on_device(): call(functools.partial(flow_kernel, s, distances), shape((s.piece, s.topi...  0.98 us
  transfers between devices with their start and end apart: 10, of which 3 were waited for; matrix products, arithmetic and copies ran while one was open for 0% of the time, Pallas kernels for 4%

profile of v5, /device:TPU:0, one launch (start us, length us, event | category | flops | bytes accessed | tf_op | source)
XLA Modules:
  0.0 38.0 jit_solution(14252863715055992145)
XLA Ops:
  0.0 1.6 %shard_map.64 = (bf16[8,136,128]{2,1,0:T(8,128)(2,1)S(1)}, bf16[96,128]{1,0:T(8,128)(2,1)S(1)}, bf16[64,512]{1,0:T(8,128)(2,1)S(1)}, bf16[64,512]{1,0:T(8,128)(2...) custom-call(s32[2,4]{1,0:T(2,128)} %tiles_hbm.1, bf16[256,512]{1,0:T(8,128)(2,1)} %links_hbm.1, ...), custom_call_target="tpu_custom_call" | custom-call | flops 1000000 | bytes 1000000 | tf_op jit(solution)/shard_map/pallas_call | solution.py:344
  1.6 15.3 %all_to_all.5.buffer_ref = bf16[8,136,128]{2,1,0:T(8,128)(2,1)S(1)} all-to-all(bf16[8,136,128]{2,1,0:T(8,128)(2,1)S(1)} %get-tuple-element.18), channel_id=1, replica_groups={{16,20,24,28,0,4,8,12},{17,21,25,29,1,5,9,13},{18,22,26,30,2,6,10,14},{..., dimensions={0} | all-to-all | bytes 557056 | tf_op jit(solution)/shard_map/all_to_all | solution.py:360
  16.9 0.0 copy-start
  16.9 1.6 %collective-permute-start.8 = (bf16[512,128]{1,0:T(8,128)(2,1)S(1)}, bf16[512,128]{1,0:T(8,128)(2,1)S(1)}, u32[]{:S(2)}, u32[]{:S(2)}) collective-permute-start(bf16[512,128]{1,0:T(8,128)(2,1)S(1)} %shard_map.67.local_ref.refs_0_), channel_id=1, source_target_pairs={{0,2},{1,3},{2,0},{3,1},{4,6},{5,7},{6,4},{7,5},{8,10},{9,11},{10,... | collective-permute-start | bytes 393224 | tf_op jit(solution)/shard_map/ppermute | solution.py:304
  18.5 0.0 collective-permute-start.7
  18.5 3.4 %collective-permute-done.8.refs_2_ = bf16[512,128]{1,0:T(8,128)(2,1)S(1)} collective-permute-done((bf16[512,128]{1,0:T(8,128)(2,1)S(1)}, bf16[512,128]{1,0:T(8,128)(2,1)S(1)}, u32[]{:S(2)}, u32[]{:S(2)}) %collective-permute-start.8) | collective-permute-done | bytes 131104 | tf_op jit(solution)/shard_map/ppermute | solution.py:304
  22.0 0.0 collective-permute-start.9
  22.0 0.7 %collective-permute-start = (bf16[96,128]{1,0:T(8,128)(2,1)S(1)}, bf16[96,128]{1,0:T(8,128)(2,1)S(1)}, u32[]{:S(2)}, u32[]{:S(2)}) collective-permute-start(bf16[96,128]{1,0:T(8,128)(2,1)S(1)} %get-tuple-element.13), channel_id=1, source_target_pairs={{0,0},{1,8},{2,16},{3,24},{4,1},{5,9},{6,17},{7,25},{8,2},{9,10},{... | collective-permute-start | bytes 73736 | tf_op jit(solution)/shard_map/ppermute | solution.py:357
  22.6 2.0 %collective-permute-start.1 = (bf16[64,512]{1,0:T(8,128)(2,1)S(1)}, bf16[64,512]{1,0:T(8,128)(2,1)S(1)}, u32[]{:S(2)}, u32[]{:S(2)}) collective-permute-start(bf16[64,512]{1,0:T(8,128)(2,1)S(1)} %get-tuple-element.15), channel_id=1, source_target_pairs={{0,1},{1,0},{2,3},{3,2},{4,5},{5,4},{6,7},{7,6},{8,9},{9,8},{10,11... | collective-permute-start | bytes 196616 | tf_op jit(solution)/shard_map/ppermute | solution.py:304
  24.7 3.2 %collective-permute-start.2 = (bf16[64,512]{1,0:T(8,128)(2,1)S(1)}, bf16[64,512]{1,0:T(8,128)(2,1)S(1)}, u32[]{:S(2)}, u32[]{:S(2)}) collective-permute-start(bf16[64,512]{1,0:T(8,128)(2,1)S(1)} %get-tuple-element.16), channel_id=1, source_target_pairs={{0,2},{1,3},{2,0},{3,1},{4,6},{5,7},{6,4},{7,5},{8,10},{9,11},{10,... | collective-permute-start | bytes 196616 | tf_op jit(solution)/shard_map/ppermute | solution.py:304
  27.9 0.0 collective-permute-done.own_ref
  27.9 0.0 copy-start.1
  27.9 2.7 %collective-permute-start.3 = (bf16[64,512]{1,0:T(8,128)(2,1)S(1)}, bf16[64,512]{1,0:T(8,128)(2,1)S(1)}, u32[]{:S(2)}, u32[]{:S(2)}) collective-permute-start(bf16[64,512]{1,0:T(8,128)(2,1)S(1)} %get-tuple-element.17), channel_id=1, source_target_pairs={{0,3},{1,2},{2,1},{3,0},{4,7},{5,6},{6,5},{7,4},{8,11},{9,10},{10,... | collective-permute-start | bytes 196616 | tf_op jit(solution)/shard_map/ppermute | solution.py:304
  30.6 0.0 copy-done
  30.6 0.3 shard_map.68.refs_0_
  30.9 0.0 collective-permute-done.1.refs_1_
  30.9 0.1 collective-permute-start.4
  31.0 0.0 collective-permute-done.2.refs_2_
  31.0 1.2 %collective-permute-start.5 = (bf16[48,128]{1,0:T(8,128)(2,1)S(1)}, bf16[48,128]{1,0:T(8,128)(2,1)S(1)}, u32[]{:S(2)}, u32[]{:S(2)}) collective-permute-start(bf16[48,128]{1,0:T(8,128)(2,1)S(1)} %shard_map.68.refs_0_), channel_id=1, source_target_pairs={{0,2},{1,3},{2,0},{3,1},{4,6},{5,7},{6,4},{7,5},{8,10},{9,11},{10,... | collective-permute-start | bytes 36872 | tf_op jit(solution)/shard_map/ppermute | solution.py:304
  32.2 1.0 %collective-permute-done.3.refs_3_ = bf16[64,512]{1,0:T(8,128)(2,1)S(1)} collective-permute-done((bf16[64,512]{1,0:T(8,128)(2,1)S(1)}, bf16[64,512]{1,0:T(8,128)(2,1)S(1)}, u32[]{:S(2)}, u32[]{:S(2)}) %collective-permute-start.3) | collective-permute-done | bytes 65568 | tf_op jit(solution)/shard_map/ppermute | solution.py:304
  33.3 1.2 %collective-permute-start.6 = (bf16[48,128]{1,0:T(8,128)(2,1)S(1)}, bf16[48,128]{1,0:T(8,128)(2,1)S(1)}, u32[]{:S(2)}, u32[]{:S(2)}) collective-permute-start(bf16[48,128]{1,0:T(8,128)(2,1)S(1)} %shard_map.68.refs_0_), channel_id=1, source_target_pairs={{0,3},{1,2},{2,1},{3,0},{4,7},{5,6},{6,5},{7,4},{8,11},{9,10},{10,... | collective-permute-start | bytes 36872 | tf_op jit(solution)/shard_map/ppermute | solution.py:304
  34.5 0.0 copy-done.1
  34.5 0.3 shard_map.65.mask_ref
  34.7 0.1 shard_map.66.edges_ref
  34.8 0.0 collective-permute-done.4.refs_1_
  34.8 0.0 collective-permute-done.5.refs_2_
  34.8 1.6 %collective-permute-done.6.refs_3_ = bf16[48,128]{1,0:T(8,128)(2,1)S(1)} collective-permute-done((bf16[48,128]{1,0:T(8,128)(2,1)S(1)}, bf16[48,128]{1,0:T(8,128)(2,1)S(1)}, u32[]{:S(2)}, u32[]{:S(2)}) %collective-permute-start.6) | collective-permute-done | bytes 12320 | tf_op jit(solution)/shard_map/ppermute | solution.py:304
  36.4 0.6 %shard_map.69 = (bf16[64,2048]{1,0:T(8,128)(2,1)S(1)}, f32[64,128]{1,0:T(8,128)S(1)}) custom-call(bf16[96,128]{1,0:T(8,128)(2,1)S(1)} %collective-permute-done.own_ref, s32[16,128]{1,0:T(8,128)S(1)} %bitcast.5, bf16[64,2048]{1,0:T(8,128)(2,1)S(1)} %shard_map.66.edges_ref, bf16[48,128]{1,0:T(8,128)(2,1)S(1)} %shard_map.68.refs_0_, ...), custom_call_target="tpu_custom_call" | custom-call | flops 1000000 | bytes 1000000 | tf_op jit(solution)/shard_map/pallas_call | solution.py:377
  37.0 0.0 collective-permute-done.7.refs_1_
  37.0 0.2 shard_map.70.base_ref
  37.2 0.0 collective-permute-done.9.refs_0_
  37.2 0.8 %shard_map.71 = f32[64,128]{1,0:T(8,128)} custom-call(bf16[64,2048]{1,0:T(8,128)(2,1)S(1)} %get-tuple-element.19.weighted_ref, f32[64,128]{1,0:T(8,128)S(1)} %shard_map.70.base_ref, bf16[512,128]{1,0:T(8,128)(2,1)S(1)} %collective-permute-done.9.refs_0_), custom_call_target="tpu_custom_call" | custom-call | flops 1000000 | bytes 1000000 | tf_op jit(solution)/shard_map/pallas_call | solution.py:387
  (1 shorter events, 0.0 us)
Async XLA Ops:
  16.9 13.7 %copy-start = (s32[2048]{0:T(1024)S(1)}, s32[2048]{0:T(1024)}, u32[]{:S(2)}) copy-start(s32[2048]{0:T(1024)} %param.9) | copy-start | bytes 24580
  16.9 5.0 %collective-permute-start.8 = (bf16[512,128]{1,0:T(8,128)(2,1)S(1)}, bf16[512,128]{1,0:T(8,128)(2,1)S(1)}, u32[]{:S(2)}, u32[]{:S(2)}) collective-permute-start(bf16[512,128]{1,0:T(8,128)(2,1)S(1)} %shard_map.67.local_ref.refs_0_), channel_id=1, source_target_pairs={{0,2},{1,3},{2,0},{3,1},{4,6},{5,7},{6,4},{7,5},{8,10},{9,11},{10,... | collective-permute-start | bytes 393224 | tf_op jit(solution)/shard_map/ppermute | solution.py:304
  18.5 18.4 %collective-permute-start.7 = (bf16[512,128]{1,0:T(8,128)(2,1)S(1)}, bf16[512,128]{1,0:T(8,128)(2,1)S(1)}, u32[]{:S(2)}, u32[]{:S(2)}) collective-permute-start(bf16[512,128]{1,0:T(8,128)(2,1)S(1)} %shard_map.67.local_ref.refs_0_), channel_id=1, source_target_pairs={{0,1},{1,0},{2,3},{3,2},{4,5},{5,4},{6,7},{7,6},{8,9},{9,8},{10,11... | collective-permute-start | bytes 393224 | tf_op jit(solution)/shard_map/ppermute | solution.py:304
  22.0 15.2 %collective-permute-start.9 = (bf16[512,128]{1,0:T(8,128)(2,1)S(1)}, bf16[512,128]{1,0:T(8,128)(2,1)S(1)}, u32[]{:S(2)}, u32[]{:S(2)}) collective-permute-start(bf16[512,128]{1,0:T(8,128)(2,1)S(1)} %collective-permute-done.8.refs_2_), channel_id=1, source_target_pairs={{0,1},{1,0},{2,3},{3,2},{4,5},{5,4},{6,7},{7,6},{8,9},{9,8},{10,11... | collective-permute-start | bytes 393224 | tf_op jit(solution)/shard_map/ppermute | solution.py:304
  22.0 5.9 %collective-permute-start = (bf16[96,128]{1,0:T(8,128)(2,1)S(1)}, bf16[96,128]{1,0:T(8,128)(2,1)S(1)}, u32[]{:S(2)}, u32[]{:S(2)}) collective-permute-start(bf16[96,128]{1,0:T(8,128)(2,1)S(1)} %get-tuple-element.13), channel_id=1, source_target_pairs={{0,0},{1,8},{2,16},{3,24},{4,1},{5,9},{6,17},{7,25},{8,2},{9,10},{... | collective-permute-start | bytes 73736 | tf_op jit(solution)/shard_map/ppermute | solution.py:357
  22.6 8.3 %collective-permute-start.1 = (bf16[64,512]{1,0:T(8,128)(2,1)S(1)}, bf16[64,512]{1,0:T(8,128)(2,1)S(1)}, u32[]{:S(2)}, u32[]{:S(2)}) collective-permute-start(bf16[64,512]{1,0:T(8,128)(2,1)S(1)} %get-tuple-element.15), channel_id=1, source_target_pairs={{0,1},{1,0},{2,3},{3,2},{4,5},{5,4},{6,7},{7,6},{8,9},{9,8},{10,11... | collective-permute-start | bytes 196616 | tf_op jit(solution)/shard_map/ppermute | solution.py:304
  24.7 6.3 %collective-permute-start.2 = (bf16[64,512]{1,0:T(8,128)(2,1)S(1)}, bf16[64,512]{1,0:T(8,128)(2,1)S(1)}, u32[]{:S(2)}, u32[]{:S(2)}) collective-permute-start(bf16[64,512]{1,0:T(8,128)(2,1)S(1)} %get-tuple-element.16), channel_id=1, source_target_pairs={{0,2},{1,3},{2,0},{3,1},{4,6},{5,7},{6,4},{7,5},{8,10},{9,11},{10,... | collective-permute-start | bytes 196616 | tf_op jit(solution)/shard_map/ppermute | solution.py:304
  27.9 6.6 %copy-start.1 = (s32[2048]{0:T(1024)S(1)}, s32[2048]{0:T(1024)}, u32[]{:S(2)}) copy-start(s32[2048]{0:T(1024)} %param.10) | copy-start | bytes 24580
  27.9 5.4 %collective-permute-start.3 = (bf16[64,512]{1,0:T(8,128)(2,1)S(1)}, bf16[64,512]{1,0:T(8,128)(2,1)S(1)}, u32[]{:S(2)}, u32[]{:S(2)}) collective-permute-start(bf16[64,512]{1,0:T(8,128)(2,1)S(1)} %get-tuple-element.17), channel_id=1, source_target_pairs={{0,3},{1,2},{2,1},{3,0},{4,7},{5,6},{6,5},{7,4},{8,11},{9,10},{10,... | collective-permute-start | bytes 196616 | tf_op jit(solution)/shard_map/ppermute | solution.py:304
  30.9 3.9 %collective-permute-start.4 = (bf16[48,128]{1,0:T(8,128)(2,1)S(1)}, bf16[48,128]{1,0:T(8,128)(2,1)S(1)}, u32[]{:S(2)}, u32[]{:S(2)}) collective-permute-start(bf16[48,128]{1,0:T(8,128)(2,1)S(1)} %shard_map.68.refs_0_), channel_id=1, source_target_pairs={{0,1},{1,0},{2,3},{3,2},{4,5},{5,4},{6,7},{7,6},{8,9},{9,8},{10,11... | collective-permute-start | bytes 36872 | tf_op jit(solution)/shard_map/ppermute | solution.py:304
  31.0 3.8 %collective-permute-start.5 = (bf16[48,128]{1,0:T(8,128)(2,1)S(1)}, bf16[48,128]{1,0:T(8,128)(2,1)S(1)}, u32[]{:S(2)}, u32[]{:S(2)}) collective-permute-start(bf16[48,128]{1,0:T(8,128)(2,1)S(1)} %shard_map.68.refs_0_), channel_id=1, source_target_pairs={{0,2},{1,3},{2,0},{3,1},{4,6},{5,7},{6,4},{7,5},{8,10},{9,11},{10,... | collective-permute-start | bytes 36872 | tf_op jit(solution)/shard_map/ppermute | solution.py:304
  33.3 3.1 %collective-permute-start.6 = (bf16[48,128]{1,0:T(8,128)(2,1)S(1)}, bf16[48,128]{1,0:T(8,128)(2,1)S(1)}, u32[]{:S(2)}, u32[]{:S(2)}) collective-permute-start(bf16[48,128]{1,0:T(8,128)(2,1)S(1)} %shard_map.68.refs_0_), channel_id=1, source_target_pairs={{0,3},{1,2},{2,1},{3,0},{4,7},{5,6},{6,5},{7,4},{8,11},{9,10},{10,... | collective-permute-start | bytes 36872 | tf_op jit(solution)/shard_map/ppermute | solution.py:304

commit v6 on v5

--- a/solution.py
+++ b/solution.py
@@ -12,6 +12,7 @@
 LOCAL_ITERS = 2
 HOST_ITERS = 3
 LANES = 128
+ROW_ORDERS = {8: (4, 0, 7, 5, 3, 1, 6, 2)}
 GRANT = 24 * 2**20
 
 damping = 0.85
@@ -68,10 +69,11 @@
         self.extra = (2 * self.units + 2 + 15) // 16 * 16
 
     def row_at(self, place):
-        return (place + self.rows // 2) % self.rows
+        listed = ROW_ORDERS.get(self.rows)
+        return listed[place] if listed else (place + self.rows // 2) % self.rows
 
     def place_of(self, row):
-        return (row - self.rows // 2) % self.rows
+        return [self.row_at(place) for place in range(self.rows)].index(row)
 
 
 def rows_of(row, half, piece):

time: 38.2 us -> 38.2 us (level)
  no operation moved by 1% of the time
where the time goes in v6:
time: 38.2 us; the launch traced here: 38 us
  blocking collectives  15.3 us (40%)
  starting transfers between devices  12.8 us (34%)
  waiting for transfers between devices  6.05 us (16%)
  Pallas kernels  3.72 us (10%)
    all_to_all x1, blocking collectives, on_device(): lax.all_to_all(sent, 'row', 0, 0, tiled=True, axis_index_groups=[group])  15.3 us
    ppermute x9, starting transfers between devices, swap(): return lax.ppermute(x, 'col', [(i, i ^ bits) for i in range(count)])  12.1 us
    ppermute x9, waiting for transfers between devices, swap(): return lax.ppermute(x, 'col', [(i, i ^ bits) for i in range(count)])  6.05 us
    pallas_call x1, Pallas kernels, on_device(): call(functools.partial(first_kernel, s), (shape((rows, s.payload, LANES),...  1.58 us
    pallas_call x2, Pallas kernels, on_device(): call(functools.partial(flow_kernel, s, distances), shape((s.piece, s.topi...  0.98 us
  transfers between devices with their start and end apart: 10, of which 3 were waited for; matrix products, arithmetic and copies ran while one was open for 0% of the time, Pallas kernels for 4%

profile of v6, /device:TPU:0, one launch (start us, length us, event | category | flops | bytes accessed | tf_op | source)
XLA Modules:
  0.0 38.0 jit_solution(16403499801031863356)
XLA Ops:
  0.0 1.6 %shard_map.64 = (bf16[8,136,128]{2,1,0:T(8,128)(2,1)S(1)}, bf16[96,128]{1,0:T(8,128)(2,1)S(1)}, bf16[64,512]{1,0:T(8,128)(2,1)S(1)}, bf16[64,512]{1,0:T(8,128)(2...) custom-call(s32[2,4]{1,0:T(2,128)} %tiles_hbm.1, bf16[256,512]{1,0:T(8,128)(2,1)} %links_hbm.1, ...), custom_call_target="tpu_custom_call" | custom-call | flops 1000000 | bytes 1000000 | tf_op jit(solution)/shard_map/pallas_call | solution.py:346
  1.6 15.3 %all_to_all.5.buffer_ref = bf16[8,136,128]{2,1,0:T(8,128)(2,1)S(1)} all-to-all(bf16[8,136,128]{2,1,0:T(8,128)(2,1)S(1)} %get-tuple-element.18), channel_id=1, replica_groups={{16,0,28,20,12,4,24,8},{17,1,29,21,13,5,25,9},{18,2,30,22,14,6,26,10},{..., dimensions={0} | all-to-all | bytes 557056 | tf_op jit(solution)/shard_map/all_to_all | solution.py:362
  16.9 0.0 copy-start
  16.9 1.6 %collective-permute-start.8 = (bf16[512,128]{1,0:T(8,128)(2,1)S(1)}, bf16[512,128]{1,0:T(8,128)(2,1)S(1)}, u32[]{:S(2)}, u32[]{:S(2)}) collective-permute-start(bf16[512,128]{1,0:T(8,128)(2,1)S(1)} %shard_map.67.local_ref.refs_0_), channel_id=1, source_target_pairs={{0,2},{1,3},{2,0},{3,1},{4,6},{5,7},{6,4},{7,5},{8,10},{9,11},{10,... | collective-permute-start | bytes 393224 | tf_op jit(solution)/shard_map/ppermute | solution.py:306
  18.5 0.0 collective-permute-start.7
  18.5 3.4 %collective-permute-done.8.refs_2_ = bf16[512,128]{1,0:T(8,128)(2,1)S(1)} collective-permute-done((bf16[512,128]{1,0:T(8,128)(2,1)S(1)}, bf16[512,128]{1,0:T(8,128)(2,1)S(1)}, u32[]{:S(2)}, u32[]{:S(2)}) %collective-permute-start.8) | collective-permute-done | bytes 131104 | tf_op jit(solution)/shard_map/ppermute | solution.py:306
  22.0 0.0 collective-permute-start.9
  22.0 0.7 %collective-permute-start = (bf16[96,128]{1,0:T(8,128)(2,1)S(1)}, bf16[96,128]{1,0:T(8,128)(2,1)S(1)}, u32[]{:S(2)}, u32[]{:S(2)}) collective-permute-start(bf16[96,128]{1,0:T(8,128)(2,1)S(1)} %get-tuple-element.13), channel_id=1, source_target_pairs={{0,0},{1,8},{2,16},{3,24},{4,1},{5,9},{6,17},{7,25},{8,2},{9,10},{... | collective-permute-start | bytes 73736 | tf_op jit(solution)/shard_map/ppermute | solution.py:359
  22.6 2.1 %collective-permute-start.1 = (bf16[64,512]{1,0:T(8,128)(2,1)S(1)}, bf16[64,512]{1,0:T(8,128)(2,1)S(1)}, u32[]{:S(2)}, u32[]{:S(2)}) collective-permute-start(bf16[64,512]{1,0:T(8,128)(2,1)S(1)} %get-tuple-element.15), channel_id=1, source_target_pairs={{0,1},{1,0},{2,3},{3,2},{4,5},{5,4},{6,7},{7,6},{8,9},{9,8},{10,11... | collective-permute-start | bytes 196616 | tf_op jit(solution)/shard_map/ppermute | solution.py:306
  24.7 3.2 %collective-permute-start.2 = (bf16[64,512]{1,0:T(8,128)(2,1)S(1)}, bf16[64,512]{1,0:T(8,128)(2,1)S(1)}, u32[]{:S(2)}, u32[]{:S(2)}) collective-permute-start(bf16[64,512]{1,0:T(8,128)(2,1)S(1)} %get-tuple-element.16), channel_id=1, source_target_pairs={{0,2},{1,3},{2,0},{3,1},{4,6},{5,7},{6,4},{7,5},{8,10},{9,11},{10,... | collective-permute-start | bytes 196616 | tf_op jit(solution)/shard_map/ppermute | solution.py:306
  27.9 0.0 collective-permute-done.own_ref
  27.9 0.0 copy-start.1
  27.9 2.7 %collective-permute-start.3 = (bf16[64,512]{1,0:T(8,128)(2,1)S(1)}, bf16[64,512]{1,0:T(8,128)(2,1)S(1)}, u32[]{:S(2)}, u32[]{:S(2)}) collective-permute-start(bf16[64,512]{1,0:T(8,128)(2,1)S(1)} %get-tuple-element.17), channel_id=1, source_target_pairs={{0,3},{1,2},{2,1},{3,0},{4,7},{5,6},{6,5},{7,4},{8,11},{9,10},{10,... | collective-permute-start | bytes 196616 | tf_op jit(solution)/shard_map/ppermute | solution.py:306
  30.6 0.0 copy-done
  30.7 0.3 shard_map.68.refs_0_
  30.9 0.0 collective-permute-done.1.refs_1_
  30.9 0.1 collective-permute-start.4
  31.0 0.0 collective-permute-done.2.refs_2_
  31.0 1.3 %collective-permute-start.5 = (bf16[48,128]{1,0:T(8,128)(2,1)S(1)}, bf16[48,128]{1,0:T(8,128)(2,1)S(1)}, u32[]{:S(2)}, u32[]{:S(2)}) collective-permute-start(bf16[48,128]{1,0:T(8,128)(2,1)S(1)} %shard_map.68.refs_0_), channel_id=1, source_target_pairs={{0,2},{1,3},{2,0},{3,1},{4,6},{5,7},{6,4},{7,5},{8,10},{9,11},{10,... | collective-permute-start | bytes 36872 | tf_op jit(solution)/shard_map/ppermute | solution.py:306
  32.3 1.0 %collective-permute-done.3.refs_3_ = bf16[64,512]{1,0:T(8,128)(2,1)S(1)} collective-permute-done((bf16[64,512]{1,0:T(8,128)(2,1)S(1)}, bf16[64,512]{1,0:T(8,128)(2,1)S(1)}, u32[]{:S(2)}, u32[]{:S(2)}) %collective-permute-start.3) | collective-permute-done | bytes 65568 | tf_op jit(solution)/shard_map/ppermute | solution.py:306
  33.3 1.2 %collective-permute-start.6 = (bf16[48,128]{1,0:T(8,128)(2,1)S(1)}, bf16[48,128]{1,0:T(8,128)(2,1)S(1)}, u32[]{:S(2)}, u32[]{:S(2)}) collective-permute-start(bf16[48,128]{1,0:T(8,128)(2,1)S(1)} %shard_map.68.refs_0_), channel_id=1, source_target_pairs={{0,3},{1,2},{2,1},{3,0},{4,7},{5,6},{6,5},{7,4},{8,11},{9,10},{10,... | collective-permute-start | bytes 36872 | tf_op jit(solution)/shard_map/ppermute | solution.py:306
  34.5 0.0 copy-done.1
  34.5 0.3 shard_map.65.mask_ref
  34.7 0.1 shard_map.66.edges_ref
  34.8 0.0 collective-permute-done.4.refs_1_
  34.8 0.0 collective-permute-done.5.refs_2_
  34.8 1.6 %collective-permute-done.6.refs_3_ = bf16[48,128]{1,0:T(8,128)(2,1)S(1)} collective-permute-done((bf16[48,128]{1,0:T(8,128)(2,1)S(1)}, bf16[48,128]{1,0:T(8,128)(2,1)S(1)}, u32[]{:S(2)}, u32[]{:S(2)}) %collective-permute-start.6) | collective-permute-done | bytes 12320 | tf_op jit(solution)/shard_map/ppermute | solution.py:306
  36.4 0.6 %shard_map.69 = (bf16[64,2048]{1,0:T(8,128)(2,1)S(1)}, f32[64,128]{1,0:T(8,128)S(1)}) custom-call(bf16[96,128]{1,0:T(8,128)(2,1)S(1)} %collective-permute-done.own_ref, s32[16,128]{1,0:T(8,128)S(1)} %bitcast.5, bf16[64,2048]{1,0:T(8,128)(2,1)S(1)} %shard_map.66.edges_ref, bf16[48,128]{1,0:T(8,128)(2,1)S(1)} %shard_map.68.refs_0_, ...), custom_call_target="tpu_custom_call" | custom-call | flops 1000000 | bytes 1000000 | tf_op jit(solution)/shard_map/pallas_call | solution.py:379
  37.0 0.0 collective-permute-done.7.refs_1_
  37.0 0.2 shard_map.70.base_ref
  37.2 0.0 collective-permute-done.9.refs_0_
  37.2 0.8 %shard_map.71 = f32[64,128]{1,0:T(8,128)} custom-call(bf16[64,2048]{1,0:T(8,128)(2,1)S(1)} %get-tuple-element.19.weighted_ref, f32[64,128]{1,0:T(8,128)S(1)} %shard_map.70.base_ref, bf16[512,128]{1,0:T(8,128)(2,1)S(1)} %collective-permute-done.9.refs_0_), custom_call_target="tpu_custom_call" | custom-call | flops 1000000 | bytes 1000000 | tf_op jit(solution)/shard_map/pallas_call | solution.py:389
  (1 shorter events, 0.0 us)
Async XLA Ops:
  16.9 13.7 %copy-start = (s32[2048]{0:T(1024)S(1)}, s32[2048]{0:T(1024)}, u32[]{:S(2)}) copy-start(s32[2048]{0:T(1024)} %param.9) | copy-start | bytes 24580
  16.9 5.0 %collective-permute-start.8 = (bf16[512,128]{1,0:T(8,128)(2,1)S(1)}, bf16[512,128]{1,0:T(8,128)(2,1)S(1)}, u32[]{:S(2)}, u32[]{:S(2)}) collective-permute-start(bf16[512,128]{1,0:T(8,128)(2,1)S(1)} %shard_map.67.local_ref.refs_0_), channel_id=1, source_target_pairs={{0,2},{1,3},{2,0},{3,1},{4,6},{5,7},{6,4},{7,5},{8,10},{9,11},{10,... | collective-permute-start | bytes 393224 | tf_op jit(solution)/shard_map/ppermute | solution.py:306
  18.5 18.4 %collective-permute-start.7 = (bf16[512,128]{1,0:T(8,128)(2,1)S(1)}, bf16[512,128]{1,0:T(8,128)(2,1)S(1)}, u32[]{:S(2)}, u32[]{:S(2)}) collective-permute-start(bf16[512,128]{1,0:T(8,128)(2,1)S(1)} %shard_map.67.local_ref.refs_0_), channel_id=1, source_target_pairs={{0,1},{1,0},{2,3},{3,2},{4,5},{5,4},{6,7},{7,6},{8,9},{9,8},{10,11... | collective-permute-start | bytes 393224 | tf_op jit(solution)/shard_map/ppermute | solution.py:306
  22.0 15.2 %collective-permute-start.9 = (bf16[512,128]{1,0:T(8,128)(2,1)S(1)}, bf16[512,128]{1,0:T(8,128)(2,1)S(1)}, u32[]{:S(2)}, u32[]{:S(2)}) collective-permute-start(bf16[512,128]{1,0:T(8,128)(2,1)S(1)} %collective-permute-done.8.refs_2_), channel_id=1, source_target_pairs={{0,1},{1,0},{2,3},{3,2},{4,5},{5,4},{6,7},{7,6},{8,9},{9,8},{10,11... | collective-permute-start | bytes 393224 | tf_op jit(solution)/shard_map/ppermute | solution.py:306
  22.0 6.0 %collective-permute-start = (bf16[96,128]{1,0:T(8,128)(2,1)S(1)}, bf16[96,128]{1,0:T(8,128)(2,1)S(1)}, u32[]{:S(2)}, u32[]{:S(2)}) collective-permute-start(bf16[96,128]{1,0:T(8,128)(2,1)S(1)} %get-tuple-element.13), channel_id=1, source_target_pairs={{0,0},{1,8},{2,16},{3,24},{4,1},{5,9},{6,17},{7,25},{8,2},{9,10},{... | collective-permute-start | bytes 73736 | tf_op jit(solution)/shard_map/ppermute | solution.py:359
  22.6 8.3 %collective-permute-start.1 = (bf16[64,512]{1,0:T(8,128)(2,1)S(1)}, bf16[64,512]{1,0:T(8,128)(2,1)S(1)}, u32[]{:S(2)}, u32[]{:S(2)}) collective-permute-start(bf16[64,512]{1,0:T(8,128)(2,1)S(1)} %get-tuple-element.15), channel_id=1, source_target_pairs={{0,1},{1,0},{2,3},{3,2},{4,5},{5,4},{6,7},{7,6},{8,9},{9,8},{10,11... | collective-permute-start | bytes 196616 | tf_op jit(solution)/shard_map/ppermute | solution.py:306
  24.7 6.3 %collective-permute-start.2 = (bf16[64,512]{1,0:T(8,128)(2,1)S(1)}, bf16[64,512]{1,0:T(8,128)(2,1)S(1)}, u32[]{:S(2)}, u32[]{:S(2)}) collective-permute-start(bf16[64,512]{1,0:T(8,128)(2,1)S(1)} %get-tuple-element.16), channel_id=1, source_target_pairs={{0,2},{1,3},{2,0},{3,1},{4,6},{5,7},{6,4},{7,5},{8,10},{9,11},{10,... | collective-permute-start | bytes 196616 | tf_op jit(solution)/shard_map/ppermute | solution.py:306
  27.9 6.5 %copy-start.1 = (s32[2048]{0:T(1024)S(1)}, s32[2048]{0:T(1024)}, u32[]{:S(2)}) copy-start(s32[2048]{0:T(1024)} %param.10) | copy-start | bytes 24580
  27.9 5.3 %collective-permute-start.3 = (bf16[64,512]{1,0:T(8,128)(2,1)S(1)}, bf16[64,512]{1,0:T(8,128)(2,1)S(1)}, u32[]{:S(2)}, u32[]{:S(2)}) collective-permute-start(bf16[64,512]{1,0:T(8,128)(2,1)S(1)} %get-tuple-element.17), channel_id=1, source_target_pairs={{0,3},{1,2},{2,1},{3,0},{4,7},{5,6},{6,5},{7,4},{8,11},{9,10},{10,... | collective-permute-start | bytes 196616 | tf_op jit(solution)/shard_map/ppermute | solution.py:306
  30.9 3.9 %collective-permute-start.4 = (bf16[48,128]{1,0:T(8,128)(2,1)S(1)}, bf16[48,128]{1,0:T(8,128)(2,1)S(1)}, u32[]{:S(2)}, u32[]{:S(2)}) collective-permute-start(bf16[48,128]{1,0:T(8,128)(2,1)S(1)} %shard_map.68.refs_0_), channel_id=1, source_target_pairs={{0,1},{1,0},{2,3},{3,2},{4,5},{5,4},{6,7},{7,6},{8,9},{9,8},{10,11... | collective-permute-start | bytes 36872 | tf_op jit(solution)/shard_map/ppermute | solution.py:306
  31.0 3.8 %collective-permute-start.5 = (bf16[48,128]{1,0:T(8,128)(2,1)S(1)}, bf16[48,128]{1,0:T(8,128)(2,1)S(1)}, u32[]{:S(2)}, u32[]{:S(2)}) collective-permute-start(bf16[48,128]{1,0:T(8,128)(2,1)S(1)} %shard_map.68.refs_0_), channel_id=1, source_target_pairs={{0,2},{1,3},{2,0},{3,1},{4,6},{5,7},{6,4},{7,5},{8,10},{9,11},{10,... | collective-permute-start | bytes 36872 | tf_op jit(solution)/shard_map/ppermute | solution.py:306
  33.3 3.1 %collective-permute-start.6 = (bf16[48,128]{1,0:T(8,128)(2,1)S(1)}, bf16[48,128]{1,0:T(8,128)(2,1)S(1)}, u32[]{:S(2)}, u32[]{:S(2)}) collective-permute-start(bf16[48,128]{1,0:T(8,128)(2,1)S(1)} %shard_map.68.refs_0_), channel_id=1, source_target_pairs={{0,3},{1,2},{2,1},{3,0},{4,7},{5,6},{6,5},{7,4},{8,11},{9,10},{10,... | collective-permute-start | bytes 36872 | tf_op jit(solution)/shard_map/ppermute | solution.py:306

commit v7 on v6

--- a/solution.py
+++ b/solution.py
@@ -85,8 +85,9 @@
 
 
 def first_kernel(s, tiles_hbm, links_hbm, hosts_hbm, dangling_hbm, local_hbm, teleport_hbm, *refs):
-    sent_ref, own_ref, chunk_refs = refs[0], refs[1], refs[2 : 2 + s.cols]
-    tiles_ref, links_ref, hosts_ref, dangling_ref, local_ref, teleport_ref, sem = refs[2 + s.cols :]
+    sent_hbm, own_ref, chunk_refs = refs[0], refs[1], refs[2 : 2 + s.cols]
+    tiles_ref, links_ref, hosts_ref, dangling_ref, local_ref, teleport_ref = refs[2 + s.cols : -3]
+    values_ref, sem, sent_sem = refs[-3:]
     copies = [
         pltpu.make_async_copy(source, target, sem.at[i])
         for i, (source, target) in enumerate(
@@ -129,6 +130,15 @@
         ranks_high, ranks_low = split(ranks)
         flow = mm(high, ranks_high) + mm(high, ranks_low) + mm(low, ranks_high)
         ranks = damping * flow + (1 - damping) * restart
+    parts = (slice(0, s.piece), slice(s.piece, s.payload))
+    sends = [
+        pltpu.make_async_copy(values_ref.at[:, part], sent_hbm.at[:, part], sent_sem.at[i])
+        for i, part in enumerate(parts)
+    ]
+    ranks = ranks.astype(bf16)
+    for n in range(s.rows):
+        values_ref[n, parts[0], :] = ranks
+    sends[0].start()
     half_piece = s.piece // 2
     packed = jnp.concatenate([local[:half_piece], local[half_piece:]], axis=1).astype(bf16)
     own_ref[: s.piece, :] = tele_high
@@ -154,6 +164,12 @@
             stored = (tiles_ref[a, b] > 0).astype(f32)
             part = sums[:, b * s.tile : (b + 1) * s.tile]
             counts[b].append(jnp.where(valid, part, 0.0) * stored)
+    values = jnp.concatenate(
+        [jnp.concatenate(c, axis=0).astype(bf16) for c in counts] + [extra.astype(bf16)], axis=0
+    )
+    for n in range(s.rows):
+        values_ref[n, parts[1], :] = values
+    sends[1].start()
     for k in range(s.cols):
         chunk = column ^ k
         at = pl.multiple_of(chunk * s.piece, s.piece)
@@ -161,14 +177,8 @@
             lanes = slice(b * s.tile, (b + 1) * s.tile)
             stored = (tiles_ref[chunk // s.pair, b] > 0).astype(f32).astype(bf16)
             chunk_refs[k][:, lanes] = links_ref[pl.ds(at, s.piece), lanes] * stored
-    values = jnp.concatenate(
-        [ranks.astype(bf16)]
-        + [jnp.concatenate(c, axis=0).astype(bf16) for c in counts]
-        + [extra.astype(bf16)],
-        axis=0,
-    )
-    for n in range(s.rows):
-        sent_ref[n] = values
+    for copy in sends:
+        copy.wait()
 
 
 def ranks_kernel(s, buffer_ref, local_ref):
@@ -323,13 +333,14 @@
     return found
 
 
-def call(kernel, out_shape, in_specs, scratch=(), cost=10**6):
-    single = not isinstance(out_shape, tuple)
+def call(kernel, out_shape, in_specs, scratch=(), cost=10**6, out_specs=None):
+    if out_specs is None:
+        out_specs = (VMEM,) * len(out_shape) if isinstance(out_shape, tuple) else VMEM
     return pl.pallas_call(
         kernel,
         out_shape=out_shape,
         in_specs=in_specs,
-        out_specs=VMEM if single else (VMEM,) * len(out_shape),
+        out_specs=out_specs,
         scratch_shapes=scratch,
         compiler_params=pltpu.CompilerParams(vmem_limit_bytes=GRANT),
         cost_estimate=pl.CostEstimate(flops=cost, bytes_accessed=cost, transcendentals=0),
@@ -346,14 +357,16 @@
     sent, own, *chunks = call(
         functools.partial(first_kernel, s),
         (
-            shape((rows, s.payload, LANES), bf16),
+            pltpu.HBM((rows, s.payload, LANES), bf16),
             shape((s.piece + s.packed, LANES), bf16),
             *(shape((s.piece, s.width), bf16) for _ in range(cols)),
         ),
         [HBM] * 6,
         [pltpu.SMEM(tiles.shape, tiles.dtype)]
         + [pltpu.VMEM(a.shape, a.dtype) for a in (links, hosts, ignored, local_links, teleport)]
-        + [pltpu.SemaphoreType.DMA((6,))],
+        + [pltpu.VMEM((rows, s.payload, LANES), bf16)]
+        + [pltpu.SemaphoreType.DMA((6,)), pltpu.SemaphoreType.DMA((2,))],
+        out_specs=(HBM,) + (VMEM,) * (1 + cols),
     )(*(in_hbm(x) for x in (tiles, links, hosts, ignored, local_links, teleport)))
     moves = [(r * cols + c, c * rows + r) for r in range(rows) for c in range(cols)]
     own = lax.ppermute(own, ("row", "col"), moves)

time: 38.2 us -> 39.1 us (1.024)
  Pallas kernels: 3.72 us -> 4.4 us
    pallas_call x1, Pallas kernels: 1.58 us -> 2.26 us  [on_device(): call(functools.partial(first_kernel, s), (pltpu.HBM((rows, s.payload, LAN...]
  transfers between devices with their start and end apart: 10 -> 10, of which waited for: 3 -> 3; matrix products, arithmetic and copies ran while one was open for 0% -> 0% of each run, Pallas kernels for 4% -> 3%
where the time goes in v7:
time: 39.1 us; the launch traced here: 38.9 us
  blocking collectives  15.5 us (40%)
  starting transfers between devices  12.8 us (33%)
  waiting for transfers between devices  6.05 us (15%)
  Pallas kernels  4.4 us (11%)
    all_to_all x1, blocking collectives, on_device(): lax.all_to_all(sent, 'row', 0, 0, tiled=True, axis_index_groups=[group])  15.5 us
    ppermute x9, starting transfers between devices, swap(): return lax.ppermute(x, 'col', [(i, i ^ bits) for i in range(count)])  12.1 us
    ppermute x9, waiting for transfers between devices, swap(): return lax.ppermute(x, 'col', [(i, i ^ bits) for i in range(count)])  6.05 us
    pallas_call x1, Pallas kernels, on_device(): call(functools.partial(first_kernel, s), (pltpu.HBM((rows, s.payload, LAN...  2.26 us
    pallas_call x2, Pallas kernels, on_device(): call(functools.partial(flow_kernel, s, distances), shape((s.piece, s.topi...  0.98 us
  transfers between devices with their start and end apart: 10, of which 3 were waited for; matrix products, arithmetic and copies ran while one was open for 0% of the time, Pallas kernels for 3%

profile of v7, /device:TPU:0, one launch (start us, length us, event | category | flops | bytes accessed | tf_op | source)
XLA Modules:
  0.0 38.9 jit_solution(3485920635346468642)
XLA Ops:
  0.0 2.3 %shard_map.64 = (bf16[8,136,128]{2,1,0:T(8,128)(2,1)}, bf16[96,128]{1,0:T(8,128)(2,1)S(1)}, bf16[64,512]{1,0:T(8,128)(2,1)S(1)}, bf16[64,512]{1,0:T(8,128)(2,1)S...) custom-call(s32[2,4]{1,0:T(2,128)} %tiles_hbm.1, bf16[256,512]{1,0:T(8,128)(2,1)} %links_hbm.1, ...), custom_call_target="tpu_custom_call" | custom-call | flops 1000000 | bytes 1000000 | tf_op jit(solution)/shard_map/pallas_call | solution.py:357
  2.3 15.5 %all_to_all.5.buffer_ref = bf16[8,136,128]{2,1,0:T(8,128)(2,1)S(1)} all-to-all(bf16[8,136,128]{2,1,0:T(8,128)(2,1)} %get-tuple-element.18), channel_id=1, replica_groups={{16,0,28,20,12,4,24,8},{17,1,29,21,13,5,25,9},{18,2,30,22,14,6,26,10},{..., dimensions={0} | all-to-all | bytes 557056 | tf_op jit(solution)/shard_map/all_to_all | solution.py:375
  17.8 0.0 copy-start
  17.8 1.6 %collective-permute-start.8 = (bf16[512,128]{1,0:T(8,128)(2,1)S(1)}, bf16[512,128]{1,0:T(8,128)(2,1)S(1)}, u32[]{:S(2)}, u32[]{:S(2)}) collective-permute-start(bf16[512,128]{1,0:T(8,128)(2,1)S(1)} %shard_map.67.local_ref.refs_0_), channel_id=1, source_target_pairs={{0,2},{1,3},{2,0},{3,1},{4,6},{5,7},{6,4},{7,5},{8,10},{9,11},{10,... | collective-permute-start | bytes 393224 | tf_op jit(solution)/shard_map/ppermute | solution.py:316
  19.4 0.0 collective-permute-start.7
  19.4 3.4 %collective-permute-done.8.refs_2_ = bf16[512,128]{1,0:T(8,128)(2,1)S(1)} collective-permute-done((bf16[512,128]{1,0:T(8,128)(2,1)S(1)}, bf16[512,128]{1,0:T(8,128)(2,1)S(1)}, u32[]{:S(2)}, u32[]{:S(2)}) %collective-permute-start.8) | collective-permute-done | bytes 131104 | tf_op jit(solution)/shard_map/ppermute | solution.py:316
  22.9 0.0 collective-permute-start.9
  22.9 0.7 %collective-permute-start = (bf16[96,128]{1,0:T(8,128)(2,1)S(1)}, bf16[96,128]{1,0:T(8,128)(2,1)S(1)}, u32[]{:S(2)}, u32[]{:S(2)}) collective-permute-start(bf16[96,128]{1,0:T(8,128)(2,1)S(1)} %get-tuple-element.13), channel_id=1, source_target_pairs={{0,0},{1,8},{2,16},{3,24},{4,1},{5,9},{6,17},{7,25},{8,2},{9,10},{... | collective-permute-start | bytes 73736 | tf_op jit(solution)/shard_map/ppermute | solution.py:372
  23.5 2.1 %collective-permute-start.1 = (bf16[64,512]{1,0:T(8,128)(2,1)S(1)}, bf16[64,512]{1,0:T(8,128)(2,1)S(1)}, u32[]{:S(2)}, u32[]{:S(2)}) collective-permute-start(bf16[64,512]{1,0:T(8,128)(2,1)S(1)} %get-tuple-element.15), channel_id=1, source_target_pairs={{0,1},{1,0},{2,3},{3,2},{4,5},{5,4},{6,7},{7,6},{8,9},{9,8},{10,11... | collective-permute-start | bytes 196616 | tf_op jit(solution)/shard_map/ppermute | solution.py:316
  25.6 3.2 %collective-permute-start.2 = (bf16[64,512]{1,0:T(8,128)(2,1)S(1)}, bf16[64,512]{1,0:T(8,128)(2,1)S(1)}, u32[]{:S(2)}, u32[]{:S(2)}) collective-permute-start(bf16[64,512]{1,0:T(8,128)(2,1)S(1)} %get-tuple-element.16), channel_id=1, source_target_pairs={{0,2},{1,3},{2,0},{3,1},{4,6},{5,7},{6,4},{7,5},{8,10},{9,11},{10,... | collective-permute-start | bytes 196616 | tf_op jit(solution)/shard_map/ppermute | solution.py:316
  28.8 0.0 collective-permute-done.own_ref
  28.8 0.0 copy-start.1
  28.8 2.7 %collective-permute-start.3 = (bf16[64,512]{1,0:T(8,128)(2,1)S(1)}, bf16[64,512]{1,0:T(8,128)(2,1)S(1)}, u32[]{:S(2)}, u32[]{:S(2)}) collective-permute-start(bf16[64,512]{1,0:T(8,128)(2,1)S(1)} %get-tuple-element.17), channel_id=1, source_target_pairs={{0,3},{1,2},{2,1},{3,0},{4,7},{5,6},{6,5},{7,4},{8,11},{9,10},{10,... | collective-permute-start | bytes 196616 | tf_op jit(solution)/shard_map/ppermute | solution.py:316
  31.5 0.0 copy-done
  31.5 0.3 shard_map.68.refs_0_
  31.8 0.0 collective-permute-done.1.refs_1_
  31.8 0.1 collective-permute-start.4
  31.9 0.0 collective-permute-done.2.refs_2_
  31.9 1.3 %collective-permute-start.5 = (bf16[48,128]{1,0:T(8,128)(2,1)S(1)}, bf16[48,128]{1,0:T(8,128)(2,1)S(1)}, u32[]{:S(2)}, u32[]{:S(2)}) collective-permute-start(bf16[48,128]{1,0:T(8,128)(2,1)S(1)} %shard_map.68.refs_0_), channel_id=1, source_target_pairs={{0,2},{1,3},{2,0},{3,1},{4,6},{5,7},{6,4},{7,5},{8,10},{9,11},{10,... | collective-permute-start | bytes 36872 | tf_op jit(solution)/shard_map/ppermute | solution.py:316
  33.2 1.0 %collective-permute-done.3.refs_3_ = bf16[64,512]{1,0:T(8,128)(2,1)S(1)} collective-permute-done((bf16[64,512]{1,0:T(8,128)(2,1)S(1)}, bf16[64,512]{1,0:T(8,128)(2,1)S(1)}, u32[]{:S(2)}, u32[]{:S(2)}) %collective-permute-start.3) | collective-permute-done | bytes 65568 | tf_op jit(solution)/shard_map/ppermute | solution.py:316
  34.2 1.2 %collective-permute-start.6 = (bf16[48,128]{1,0:T(8,128)(2,1)S(1)}, bf16[48,128]{1,0:T(8,128)(2,1)S(1)}, u32[]{:S(2)}, u32[]{:S(2)}) collective-permute-start(bf16[48,128]{1,0:T(8,128)(2,1)S(1)} %shard_map.68.refs_0_), channel_id=1, source_target_pairs={{0,3},{1,2},{2,1},{3,0},{4,7},{5,6},{6,5},{7,4},{8,11},{9,10},{10,... | collective-permute-start | bytes 36872 | tf_op jit(solution)/shard_map/ppermute | solution.py:316
  35.4 0.0 copy-done.1
  35.4 0.3 shard_map.65.mask_ref
  35.6 0.1 shard_map.66.edges_ref
  35.7 0.0 collective-permute-done.4.refs_1_
  35.7 0.0 collective-permute-done.5.refs_2_
  35.7 1.6 %collective-permute-done.6.refs_3_ = bf16[48,128]{1,0:T(8,128)(2,1)S(1)} collective-permute-done((bf16[48,128]{1,0:T(8,128)(2,1)S(1)}, bf16[48,128]{1,0:T(8,128)(2,1)S(1)}, u32[]{:S(2)}, u32[]{:S(2)}) %collective-permute-start.6) | collective-permute-done | bytes 12320 | tf_op jit(solution)/shard_map/ppermute | solution.py:316
  37.3 0.6 %shard_map.69 = (bf16[64,2048]{1,0:T(8,128)(2,1)S(1)}, f32[64,128]{1,0:T(8,128)S(1)}) custom-call(bf16[96,128]{1,0:T(8,128)(2,1)S(1)} %collective-permute-done.own_ref, s32[16,128]{1,0:T(8,128)S(1)} %bitcast.5, bf16[64,2048]{1,0:T(8,128)(2,1)S(1)} %shard_map.66.edges_ref, bf16[48,128]{1,0:T(8,128)(2,1)S(1)} %shard_map.68.refs_0_, ...), custom_call_target="tpu_custom_call" | custom-call | flops 1000000 | bytes 1000000 | tf_op jit(solution)/shard_map/pallas_call | solution.py:392
  37.9 0.0 collective-permute-done.7.refs_1_
  37.9 0.2 shard_map.70.base_ref
  38.1 0.0 collective-permute-done.9.refs_0_
  38.1 0.8 %shard_map.71 = f32[64,128]{1,0:T(8,128)} custom-call(bf16[64,2048]{1,0:T(8,128)(2,1)S(1)} %get-tuple-element.19.weighted_ref, f32[64,128]{1,0:T(8,128)S(1)} %shard_map.70.base_ref, bf16[512,128]{1,0:T(8,128)(2,1)S(1)} %collective-permute-done.9.refs_0_), custom_call_target="tpu_custom_call" | custom-call | flops 1000000 | bytes 1000000 | tf_op jit(solution)/shard_map/pallas_call | solution.py:402
  (1 shorter events, 0.0 us)
Async XLA Ops:
  17.8 13.7 %copy-start = (s32[2048]{0:T(1024)S(1)}, s32[2048]{0:T(1024)}, u32[]{:S(2)}) copy-start(s32[2048]{0:T(1024)} %param.9) | copy-start | bytes 24580
  17.8 5.0 %collective-permute-start.8 = (bf16[512,128]{1,0:T(8,128)(2,1)S(1)}, bf16[512,128]{1,0:T(8,128)(2,1)S(1)}, u32[]{:S(2)}, u32[]{:S(2)}) collective-permute-start(bf16[512,128]{1,0:T(8,128)(2,1)S(1)} %shard_map.67.local_ref.refs_0_), channel_id=1, source_target_pairs={{0,2},{1,3},{2,0},{3,1},{4,6},{5,7},{6,4},{7,5},{8,10},{9,11},{10,... | collective-permute-start | bytes 393224 | tf_op jit(solution)/shard_map/ppermute | solution.py:316
  19.4 18.4 %collective-permute-start.7 = (bf16[512,128]{1,0:T(8,128)(2,1)S(1)}, bf16[512,128]{1,0:T(8,128)(2,1)S(1)}, u32[]{:S(2)}, u32[]{:S(2)}) collective-permute-start(bf16[512,128]{1,0:T(8,128)(2,1)S(1)} %shard_map.67.local_ref.refs_0_), channel_id=1, source_target_pairs={{0,1},{1,0},{2,3},{3,2},{4,5},{5,4},{6,7},{7,6},{8,9},{9,8},{10,11... | collective-permute-start | bytes 393224 | tf_op jit(solution)/shard_map/ppermute | solution.py:316
  22.9 15.2 %collective-permute-start.9 = (bf16[512,128]{1,0:T(8,128)(2,1)S(1)}, bf16[512,128]{1,0:T(8,128)(2,1)S(1)}, u32[]{:S(2)}, u32[]{:S(2)}) collective-permute-start(bf16[512,128]{1,0:T(8,128)(2,1)S(1)} %collective-permute-done.8.refs_2_), channel_id=1, source_target_pairs={{0,1},{1,0},{2,3},{3,2},{4,5},{5,4},{6,7},{7,6},{8,9},{9,8},{10,11... | collective-permute-start | bytes 393224 | tf_op jit(solution)/shard_map/ppermute | solution.py:316
  22.9 6.0 %collective-permute-start = (bf16[96,128]{1,0:T(8,128)(2,1)S(1)}, bf16[96,128]{1,0:T(8,128)(2,1)S(1)}, u32[]{:S(2)}, u32[]{:S(2)}) collective-permute-start(bf16[96,128]{1,0:T(8,128)(2,1)S(1)} %get-tuple-element.13), channel_id=1, source_target_pairs={{0,0},{1,8},{2,16},{3,24},{4,1},{5,9},{6,17},{7,25},{8,2},{9,10},{... | collective-permute-start | bytes 73736 | tf_op jit(solution)/shard_map/ppermute | solution.py:372
  23.5 8.3 %collective-permute-start.1 = (bf16[64,512]{1,0:T(8,128)(2,1)S(1)}, bf16[64,512]{1,0:T(8,128)(2,1)S(1)}, u32[]{:S(2)}, u32[]{:S(2)}) collective-permute-start(bf16[64,512]{1,0:T(8,128)(2,1)S(1)} %get-tuple-element.15), channel_id=1, source_target_pairs={{0,1},{1,0},{2,3},{3,2},{4,5},{5,4},{6,7},{7,6},{8,9},{9,8},{10,11... | collective-permute-start | bytes 196616 | tf_op jit(solution)/shard_map/ppermute | solution.py:316
  25.6 6.3 %collective-permute-start.2 = (bf16[64,512]{1,0:T(8,128)(2,1)S(1)}, bf16[64,512]{1,0:T(8,128)(2,1)S(1)}, u32[]{:S(2)}, u32[]{:S(2)}) collective-permute-start(bf16[64,512]{1,0:T(8,128)(2,1)S(1)} %get-tuple-element.16), channel_id=1, source_target_pairs={{0,2},{1,3},{2,0},{3,1},{4,6},{5,7},{6,4},{7,5},{8,10},{9,11},{10,... | collective-permute-start | bytes 196616 | tf_op jit(solution)/shard_map/ppermute | solution.py:316
  28.8 6.5 %copy-start.1 = (s32[2048]{0:T(1024)S(1)}, s32[2048]{0:T(1024)}, u32[]{:S(2)}) copy-start(s32[2048]{0:T(1024)} %param.10) | copy-start | bytes 24580
  28.8 5.3 %collective-permute-start.3 = (bf16[64,512]{1,0:T(8,128)(2,1)S(1)}, bf16[64,512]{1,0:T(8,128)(2,1)S(1)}, u32[]{:S(2)}, u32[]{:S(2)}) collective-permute-start(bf16[64,512]{1,0:T(8,128)(2,1)S(1)} %get-tuple-element.17), channel_id=1, source_target_pairs={{0,3},{1,2},{2,1},{3,0},{4,7},{5,6},{6,5},{7,4},{8,11},{9,10},{10,... | collective-permute-start | bytes 196616 | tf_op jit(solution)/shard_map/ppermute | solution.py:316
  31.8 3.9 %collective-permute-start.4 = (bf16[48,128]{1,0:T(8,128)(2,1)S(1)}, bf16[48,128]{1,0:T(8,128)(2,1)S(1)}, u32[]{:S(2)}, u32[]{:S(2)}) collective-permute-start(bf16[48,128]{1,0:T(8,128)(2,1)S(1)} %shard_map.68.refs_0_), channel_id=1, source_target_pairs={{0,1},{1,0},{2,3},{3,2},{4,5},{5,4},{6,7},{7,6},{8,9},{9,8},{10,11... | collective-permute-start | bytes 36872 | tf_op jit(solution)/shard_map/ppermute | solution.py:316
  31.9 3.8 %collective-permute-start.5 = (bf16[48,128]{1,0:T(8,128)(2,1)S(1)}, bf16[48,128]{1,0:T(8,128)(2,1)S(1)}, u32[]{:S(2)}, u32[]{:S(2)}) collective-permute-start(bf16[48,128]{1,0:T(8,128)(2,1)S(1)} %shard_map.68.refs_0_), channel_id=1, source_target_pairs={{0,2},{1,3},{2,0},{3,1},{4,6},{5,7},{6,4},{7,5},{8,10},{9,11},{10,... | collective-permute-start | bytes 36872 | tf_op jit(solution)/shard_map/ppermute | solution.py:316
  34.2 3.1 %collective-permute-start.6 = (bf16[48,128]{1,0:T(8,128)(2,1)S(1)}, bf16[48,128]{1,0:T(8,128)(2,1)S(1)}, u32[]{:S(2)}, u32[]{:S(2)}) collective-permute-start(bf16[48,128]{1,0:T(8,128)(2,1)S(1)} %shard_map.68.refs_0_), channel_id=1, source_target_pairs={{0,3},{1,2},{2,1},{3,0},{4,7},{5,6},{6,5},{7,4},{8,11},{9,10},{10,... | collective-permute-start | bytes 36872 | tf_op jit(solution)/shard_map/ppermute | solution.py:316
